TPU v7x, 32 devices: a whole 2x2x4 slice. The times are simulated.
32 devices in a mesh: dp: 4 (over x, core), expert: 8 (over z, y).
Axes of the slice: x: 2, y: 2, z: 4, core: 2. Of those that a mesh axis runs over, the one named last changes fastest.
Arguments:
- attended: bfloat16 [4096, 1536], P(('dp', 'expert')), may hold values from -6 to 6
- residual: bfloat16 [4096, 1536], P(('dp', 'expert')), may hold values from -6 to 6
- new_kv: bfloat16 [4096, 1024], P(('dp', 'expert')), may hold values from -6 to 6
- kv_pool: bfloat16 [256, 128, 1024], P(('dp', 'expert')), may hold values from -6 to 6
- page_table: int32 [32], P(('dp', 'expert')), may hold values from 0 to 7, as said below
- out_weight: bfloat16 [1536, 1536], P(('dp', 'expert')), may hold values from -0.3125 to 0.3125
- router: bfloat16 [1536, 40], P(('dp', 'expert')), may hold values from -0.15625 to 0.15625
- attn_gain: bfloat16 [1536], P(('dp', 'expert')), may hold values from 0.099609375 to 1.8984375
- ffn_gain: bfloat16 [1536], P(('dp', 'expert')), may hold values from 0.099609375 to 1.8984375
- routes: int32 [4096, 8], P(('dp', 'expert')), may hold values from 0 to 39, all different within a row
- replica_pick: int32 [4096, 8], P(('dp', 'expert')), may hold values from 0 to 5039
- lengths: int32 [5], replicated, may hold values from 1 to 2048, 4096 in all
- slot_expert: int32 [48], replicated, may hold values from 0 to 39, as said below
- slot_capacity: int32 [48], replicated, may hold values from 16 to 32, as said below
- slot_in: bfloat16 [48, 1536, 1024], P('expert', 'dp'), may hold values from -0.15625 to 0.15625
- slot_out: bfloat16 [48, 1536, 512], P('expert', 'dp'), may hold values from -0.25 to 0.25
Outputs:
- residual_out: bfloat16 [4096, 1536], P(('dp', 'expert'))
- next_normed: bfloat16 [4096, 1536], P(('dp', 'expert'))
- pool_out: bfloat16 [256, 128, 1024], P(('dp', 'expert'))
Inputs may be any that keep to these rules, and one draw needn't show every extreme that they name: `page_table`: each device's 1 entries differ from one another. `slot_expert`: every expert is held by one slot or more. `slot_capacity`: some slot accepts exactly 32 rows. The capacities of the 6 slots of one index of expert (slots i * 6 to i * 6 + 5) sum to at most 144, and to exactly 144 for some index.
All inputs are finite; a program needn't handle non-finite values.
Results may differ from a plain program's by a relative error of at most 0.0095.
Values may be sent and summed in bfloat16 or wider, within the bound.
A program may use at most 128 MiB of HBM per device.

v0:
```python
import jax
import jax.numpy as jnp
from jax import lax
from jax.sharding import PartitionSpec as P

eps_norm = 1e-06


def rms_scale(values, gain):
    mean_sq = jnp.mean(values * values, axis=-1, keepdims=True)
    return values * lax.rsqrt(mean_sq + eps_norm) * gain.astype(jnp.float32)


def on_device(
    attended,
    residual,
    new_kv,
    kv_pool,
    page_table,
    out_weight,
    router,
    attn_gain,
    ffn_gain,
    routes,
    replica_pick,
    lengths,
    slot_expert,
    slot_capacity,
    slot_in,
    slot_out,
):
    rows_dev, row_width = attended.shape
    experts_all = router.shape[1]
    top_count = routes.shape[1]
    slots_all = slot_expert.shape[0]
    wo_piece = lax.all_gather(out_weight, ("dp", "expert"), axis=0, tiled=True)
    router_piece = lax.all_gather(router, ("dp", "expert"), axis=0, tiled=True)
    first_piece = lax.all_gather(attn_gain, ("dp", "expert"), axis=0, tiled=True)
    second_piece = lax.all_gather(ffn_gain, ("dp", "expert"), axis=0, tiled=True)
    product = jnp.dot(attended, wo_piece, preferred_element_type=jnp.float32)
    router_full = router_piece
    gain_first = first_piece
    gain_second = second_piece
    proj, router_full, gain_first, gain_second = (product, router_full, gain_first, gain_second)
    hidden = (residual.astype(jnp.float32) + proj).astype(jnp.bfloat16)
    normed = rms_scale(hidden.astype(jnp.float32), gain_first).astype(jnp.bfloat16)
    page_rows = kv_pool.shape[1]
    new_pages = new_kv.reshape(rows_dev // page_rows, page_rows, new_kv.shape[1])
    pool_out = kv_pool.at[page_table].set(new_pages)
    logits = jnp.dot(normed, router_full, preferred_element_type=jnp.float32)
    expert_iota = lax.broadcasted_iota(jnp.int32, (1, 1, experts_all), 2)
    route_hot = routes[:, :, None] == expert_iota
    picked = jnp.sum(jnp.where(route_hot, logits[:, None, :], 0.0), axis=2)
    raised = jnp.exp(picked)
    gates = raised / jnp.sum(raised, axis=1, keepdims=True)
    held = (slot_expert[None, :] == lax.broadcasted_iota(jnp.int32, (experts_all, 1), 0)).astype(
        jnp.int32
    )
    copies = jnp.sum(held, axis=1)
    rank = jnp.sum((jnp.cumsum(held, axis=1) - held) * held, axis=0)
    route_copies = jnp.sum(jnp.where(route_hot, copies[None, None, :], 0), axis=2)
    wanted = replica_pick % route_copies
    matched = (slot_expert[None, None, :] == routes[:, :, None]) & (
        rank[None, None, :] == wanted[:, :, None]
    )
    slot_iota = lax.broadcasted_iota(jnp.int32, (1, 1, slots_all), 2)
    target = jnp.sum(jnp.where(matched, slot_iota, 0), axis=2)
    live_end = jnp.sum(lengths[:-1])
    row_first = lax.axis_index(("dp", "expert")) * rows_dev
    row_ids = row_first + lax.broadcasted_iota(jnp.int32, (rows_dev, 1), 0)
    live = row_ids < live_end
    flat_target = target.reshape(-1)
    flat_live = jnp.broadcast_to(live, target.shape).reshape(-1)
    slot_hot = ((flat_target[:, None] == slot_iota[0]) & flat_live[:, None]).astype(jnp.int32)
    before = jnp.cumsum(slot_hot, axis=0) - slot_hot
    position = jnp.sum(before * slot_hot, axis=1)
    limit = jnp.sum(slot_hot * slot_capacity[None, :], axis=1)
    kept = flat_live & (position < limit)
    capacity = (rows_dev * top_count * 5 // (4 * slots_all) + 7) // 8 * 8
    holders = lax.axis_size("expert")
    slots_dev = slots_all // holders
    w_in, w_out = (
        lax.all_gather(slot_in, "dp", axis=1, tiled=True),
        lax.all_gather(slot_out, "dp", axis=1, tiled=True),
    )
    hidden_units = w_out.shape[2]
    spread_rows = jnp.repeat(normed, top_count, axis=0)
    dropped = slots_all * capacity
    place = jnp.where(kept, flat_target * capacity + position, dropped)
    send = jnp.zeros((dropped, row_width), jnp.bfloat16).at[place].set(spread_rows, mode="drop")
    outgoing = send.reshape(holders, slots_dev, capacity, row_width)
    both = jnp.einsum(
        "hscd,sdf->hscf",
        lax.all_to_all(outgoing, "expert", split_axis=0, concat_axis=0, tiled=True),
        w_in,
        preferred_element_type=jnp.float32,
    )
    inner = (jax.nn.silu(both[..., :hidden_units]) * both[..., hidden_units:]).astype(jnp.bfloat16)
    result = jnp.einsum("hscf,sdf->hscd", inner, w_out, preferred_element_type=jnp.float32).astype(
        jnp.bfloat16
    )
    back = lax.all_to_all(result, "expert", split_axis=0, concat_axis=0, tiled=True)
    fetched = back.reshape(dropped, row_width)[jnp.minimum(place, dropped - 1)]
    weighted = (
        jnp.where(kept[:, None], fetched.astype(jnp.float32), 0.0) * gates.reshape(-1)[:, None]
    )
    mixed = jnp.sum(weighted.reshape(rows_dev, top_count, row_width), axis=1)
    total = hidden.astype(jnp.float32) + mixed
    residual_out = total.astype(jnp.bfloat16)
    next_normed = rms_scale(total, gain_second).astype(jnp.bfloat16)
    return (residual_out, next_normed, pool_out)


def solution(mesh):
    in_specs = (
        P(("dp", "expert"), None),
        P(("dp", "expert"), None),
        P(("dp", "expert"), None),
        P(("dp", "expert"), None, None),
        P(("dp", "expert")),
        P(("dp", "expert"), None),
        P(("dp", "expert"), None),
        P(("dp", "expert")),
        P(("dp", "expert")),
        P(("dp", "expert"), None),
        P(("dp", "expert"), None),
        P(),
        P(),
        P(),
        P("expert", "dp", None),
        P("expert", "dp", None),
    )
    out_specs = (
        P(("dp", "expert"), None),
        P(("dp", "expert"), None),
        P(("dp", "expert"), None, None),
    )
    return jax.shard_map(
        on_device, mesh=mesh, in_specs=in_specs, out_specs=out_specs, check_vma=False
    )
```

profile of v0, /device:TPU:0, one launch (start us, length us, event | category | flops | bytes accessed | tf_op | source)
XLA Modules:
  0.0 474.5 jit_solution(535709089046775526)
XLA Ops:
  7.3 0.6 all-gather.5.cloned.1.call-update
  8.0 0.7 all-gather.7.cloned.1.call-update
  8.7 0.7 all-gather.9.cloned.1.call-update
  9.5 0.2 reduce_window_sum.26
  9.7 0.1 select_reduce_fusion.4
  9.9 0.1 add_select_fusion
  10.0 0.1 select_reduce_fusion.1
  10.1 0.1 copy.41
  10.4 0.6 slice_reduce_fusion
  11.1 0.7 add_compare_fusion.1
  11.8 0.1 and.52
  11.9 0.1 reshape.226
  12.0 0.7 add_compare_fusion
  12.8 0.1 broadcast_in_dim.96
  12.9 13.5 %reduce-window.6 = s32[48,8,128]{2,1,0:T(8,128)S(1)} reduce-window(s32[48,8,128]{2,1,0:T(8,128)S(1)} %fusion.29, s32[]{:T(128)} %constant.62.clone.1), window={size=1x1x128 pad=0_0x0_0x127_0}, to_apply=%region_6.7 | reduce-window | flops 6242304 | bytes 393220 | tf_op jit(solution)/shard_map/reduce-window
  26.4 0.1 slice.41
  26.5 0.1 copy.43
  26.8 0.1 copy.45
  26.9 0.1 mul.102
  27.0 0.2 dynamic-update-slice.3
  27.3 0.2 dynamic-update-slice.4
  27.5 42.6 %all-reduce.2 = (bf16[1536]{0:T(1024)(128)(2,1)S(1)}, bf16[1536]{0:T(1024)(128)(2,1)S(1)}) all-reduce(bf16[1536]{0:T(1024)(128)(2,1)S(1)} %dynamic-update-slice.3, bf16[1536]{0:T(1024)(128)(2,1)S(1)} %dynamic-update-slice.4), channel_id=1, replica_groups=mesh['dp'=4,'expert'=8] {'dp','expert'}, use_global_device_ids=true, to_apply=%add | all-reduce | flops 3072 | bytes 12288
  70.1 0.1 broadcast_add_fusion
  70.3 0.1 select_reduce_fusion
  70.4 7.4 %all-gather.5.cloned.1.call-done = bf16[1536,1536]{1,0:T(8,128)(2,1)} async-done(((bf16[48,1536]{1,0:T(8,128)(2,1)}), bf16[1536,1536]{1,0:T(8,128)(2,1)}) %all-gather.5.cloned.1.call-update) | async-done | bytes 4718608 | tf_op jit(solution)/shard_map/all_gather | solution.py:36
  77.8 3.2 multiply_reduce_fusion.1
  81.0 0.9 copy-done.2
  81.9 0.1 multiply_convert_fusion.1
  82.0 8.8 %scatter_custom_fusion = bf16[1536,1536]{1,0:T(8,128)(2,1)} fusion(s32[1024]{0:T(1024)S(1)} %bitcast.67, bf16[]{:T(256)} %constant.65.clone.1, bf16[128,1536]{1,0:T(8,128)(2,1)S(1)} %multiply_convert_fusion.1), kind=kCustom, calls=%fused_computation.13 | custom fusion | bytes 5111810 | tf_op jit(solution)/shard_map/scatter | solution.py:90
  90.8 109.7 %all_to_all.10 = bf16[8,6,32,1536]{3,2,1,0:T(8,128)(2,1)} all-to-all(bf16[8,6,32,1536]{3,2,1,0:T(8,128)(2,1)} %bitcast.60), channel_id=1, replica_groups=mesh['dp'=4,'expert'=8] {'expert'}, dimensions={0} | all-to-all | bytes 9437184 | tf_op jit(solution)/shard_map/all_to_all | solution.py:94
  200.5 14.1 %fusion.12 = f32[8,6,32,1024]{3,2,0,1:T(8,128)} fusion(bf16[6,1536,1024]{2,1,0:T(8,128)(2,1)} %all-gather.7.cloned.1.call-done, bf16[8,6,32,1536]{3,2,1,0:T(8,128)(2,1)} %all_to_all.10), kind=kOutput, calls=%fused_computation.15 | convolution fusion | flops 4831838208 | bytes 29884416 | tf_op jit(solution)/shard_map/hscd,sdf->hscf/dot_general | solution.py:92
  214.6 49.4 %all-gather.9.cloned.1.call-done = bf16[6,1536,512]{2,1,0:T(8,128)(2,1)} async-done(((bf16[6,384,512]{2,1,0:T(8,128)(2,1)}), bf16[6,1536,512]{2,1,0:T(8,128)(2,1)}) %all-gather.9.cloned.1.call-update) | async-done | bytes 9437200 | tf_op jit(solution)/shard_map/all_gather | solution.py:84
  264.0 10.3 %convert_bitcast_fusion = bf16[8,6,32,1536]{3,2,0,1:T(8,128)(2,1)} fusion(bf16[6,1536,512]{2,1,0:T(8,128)(2,1)} %all-gather.9.cloned.1.call-done, f32[8,6,32,1024]{3,2,0,1:T(8,128)} %fusion.12), kind=kOutput, calls=%fused_computation.10 | convolution fusion | flops 2422996992 | bytes 20447232 | tf_op jit(solution)/shard_map/hscf,sdf->hscd/dot_general | solution.py:99
  274.3 5.0 %copy.47 = bf16[8,6,32,1536]{3,2,1,0:T(8,128)(2,1)} copy(bf16[8,6,32,1536]{3,2,0,1:T(8,128)(2,1)} %convert_bitcast_fusion) | data formatting | bytes 9437184 | tf_op jit(solution)/shard_map/convert_element_type | solution.py:99
  279.4 5.7 %all-to-all-start.1 = ((bf16[8,6,32,1536]{3,2,1,0:T(8,128)(2,1)}), bf16[8,6,32,1536]{3,2,1,0:T(8,128)(2,1)}, u32[]{:S(2)}, u32[]{:S(2)}) async-start(bf16[8,6,32,1536]{3,2,1,0:T(8,128)(2,1)} %copy.47), calls=%async_computation.1 | async-start | bytes 9437184 | tf_op jit(solution)/shard_map/all_to_all | solution.py:102
  285.1 0.1 lt.76
  285.2 161.9 %all-gather = bf16[32,48,40]{1,2,0:T(8,128)(2,1)S(1)} all-gather(bf16[1,48,40]{1,2,0:T(8,128)(2,1)S(1)} %bitcast.66), channel_id=1, replica_groups=mesh['dp'=4,'expert'=8] {'dp','expert'}, dimensions={0}, use_global_device_ids=true | all-gather | bytes 126720 | tf_op jit(solution)/shard_map/all_gather | solution.py:37
  447.1 0.4 reshape.254
  447.5 0.6 convert_element_type.65
  448.7 0.7 and_reduce_fusion
  449.5 0.6 broadcast_clamp_fusion
  450.2 0.7 fusion.23
  450.9 0.2 fusion.33
  451.2 1.0 copy.49
  452.2 9.8 %gather_fusion = bf16[1024,1536]{1,0:T(8,128)(2,1)S(1)} fusion(bf16[1536,1536]{1,0:T(8,128)(2,1)} %bitcast.13, s32[1024]{0:T(1024)} %broadcast_clamp_fusion), kind=kCustom, calls=%fused_computation | custom fusion | bytes 6295552 | tf_op jit(solution)/shard_map/gather | solution.py:103
  462.0 3.6 fusion.5
  465.6 1.4 multiply_reduce_fusion
  467.0 1.0 multiply_convert_fusion
  (62 shorter events, 1.1 us)
Async XLA Ops:
  7.2 70.6 %copy-start = (bf16[128,1536]{1,0:T(8,128)(2,1)S(1)}, bf16[128,1536]{1,0:T(8,128)(2,1)}, u32[]{:S(2)}) copy-start(bf16[128,1536]{1,0:T(8,128)(2,1)} %param.18) | copy-start | bytes 1179652
  7.2 70.6 %all-gather.5.cloned.1.call-start = ((), (), s32[]{:S(2)}) async-start(), calls=%async_computation.2 | async-start | bytes 4866048 | tf_op jit(solution)/shard_map/all_gather | solution.py:36
  7.2 2.2 copy-start.10
  7.2 2.5 copy-start.7
  7.2 2.6 copy-start.11
  7.3 3.2 copy-start.14
  7.3 19.8 %copy-start.15 = (bf16[48]{0:T(256)(128)(2,1)S(1)}, bf16[48]{0:T(256)(128)(2,1)}, u32[]{:S(2)}) copy-start(bf16[48]{0:T(256)(128)(2,1)} %param.25) | copy-start | bytes 292
  7.3 20.0 %copy-start.16 = (bf16[48]{0:T(256)(128)(2,1)S(1)}, bf16[48]{0:T(256)(128)(2,1)}, u32[]{:S(2)}) copy-start(bf16[48]{0:T(256)(128)(2,1)} %param.26) | copy-start | bytes 292
  7.9 62.3 %copy-start.12 = (s32[48]{0:T(128)S(1)}, s32[48]{0:T(128)}, u32[]{:S(2)}) copy-start(s32[48]{0:T(128)} %param.31) | copy-start | bytes 580
  7.9 69.9 %copy-start.5 = (bf16[128,1536]{1,0:T(8,128)(2,1)S(1)}, bf16[128,1536]{1,0:T(8,128)(2,1)}, u32[]{:S(2)}) copy-start(bf16[128,1536]{1,0:T(8,128)(2,1)} %param.19) | copy-start | bytes 1179652
  7.9 192.6 %all-gather.7.cloned.1.call-start = ((), (), s32[]{:S(2)}) async-start(), calls=%async_computation.3 | async-start | bytes 23592960 | tf_op jit(solution)/shard_map/all_gather | solution.py:83
  8.7 255.3 %all-gather.9.cloned.1.call-start = ((), (), s32[]{:S(2)}) async-start(), calls=%async_computation.4 | async-start | bytes 11796480 | tf_op jit(solution)/shard_map/all_gather | solution.py:84
  81.0 0.9 copy-start.2
  279.4 5.8 %copy-start.9 = (bf16[48,40]{0,1:T(8,128)(2,1)S(1)}, bf16[48,40]{0,1:T(8,128)(2,1)}, u32[]{:S(2)}) copy-start(bf16[48,40]{0,1:T(8,128)(2,1)} %param.24) | copy-start | bytes 11524
  279.4 169.4 %copy-start.13 = (s32[3]{0:T(128)S(1)}, s32[3]{0:T(128)}, u32[]{:S(2)}) copy-start(s32[3]{0:T(128)} %constant.75.clone.1) | copy-start | bytes 40
  279.4 170.8 %copy-start.4 = (bf16[8,128,1024]{2,1,0:T(8,128)(2,1)S(1)}, bf16[8,128,1024]{2,1,0:T(8,128)(2,1)}, u32[]{:S(2)}) copy-start(bf16[8,128,1024]{2,1,0:T(8,128)(2,1)} %param.21) | copy-start | bytes 6291460
  279.4 170.8 %copy-start.6 = (bf16[128,1024]{1,0:T(8,128)(2,1)S(1)}, bf16[128,1024]{1,0:T(8,128)(2,1)}, u32[]{:S(2)}) copy-start(bf16[128,1024]{1,0:T(8,128)(2,1)} %param.20) | copy-start | bytes 786436
  279.4 172.8 %all-to-all-start.1 = ((bf16[8,6,32,1536]{3,2,1,0:T(8,128)(2,1)}), bf16[8,6,32,1536]{3,2,1,0:T(8,128)(2,1)}, u32[]{:S(2)}, u32[]{:S(2)}) async-start(bf16[8,6,32,1536]{3,2,1,0:T(8,128)(2,1)} %copy.47), calls=%async_computation.1 | async-start | bytes 9437184 | tf_op jit(solution)/shard_map/all_to_all | solution.py:102
  450.9 1.3 copy-start.3
  452.2 15.8 %copy-start.1 = (bf16[128,1536]{1,0:T(8,128)(2,1)S(1)}, bf16[128,1536]{1,0:T(8,128)(2,1)}, u32[]{:S(2)}) copy-start(bf16[128,1536]{1,0:T(8,128)(2,1)} %param.18) | copy-start | bytes 1179652
  462.0 5.0 %copy-start.8 = (f32[1536]{0:T(1024)S(1)}, f32[1536]{0:T(1024)}, u32[]{:S(2)}) copy-start(f32[1536]{0:T(1024)} %convert_element_type.65) | copy-start | bytes 18436
Sparse Core Ops, SparseCore 0:
  10.9 66.8 all-gather.4
  79.4 118.7 all-gather.6
  199.7 64.2 all-gather.8
where the time goes:
time: 475 us
  blocking collectives  314 us (66%)
  waiting for transfers between devices  58.7 us (12%)
  matrix products  27.9 us (6%)
  local copies, waits for them, and re-layouts  27.8 us (6%)
  other arithmetic  25.3 us (5%)
  between operations  14.8 us (3%)
  starting transfers between devices  5.77 us (1%)
    all_gather x1, blocking collectives, on_device(): router_piece = lax.all_gather(router, ('dp', 'expert'), axis=0, tiled=True)  162 us
    all_to_all x1, blocking collectives, on_device(): lax.all_to_all(outgoing, 'expert', split_axis=0, concat_axis=0, tiled=True)  110 us
    all_gather x1, waiting for transfers between devices, on_device(): lax.all_gather(slot_out, 'dp', axis=1, tiled=True)  49.4 us
    unnamed x1, blocking collectives  42.6 us
    another operation x4, other arithmetic  14.4 us
    dot_general x1, matrix products, on_device(): jnp.einsum('hscd,sdf->hscf', lax.all_to_all(outgoing, 'expert', split_axi...  14.1 us
    dot_general x1, matrix products, on_device(): jnp.einsum('hscf,sdf->hscd', inner, w_out, preferred_element_type=jnp.flo...  10.3 us
    gather x1, local copies, waits for them, and re-layouts, on_device(): fetched = back.reshape(dropped, row_width)[jnp.minimum(place, dropped - 1)]  9.78 us
  transfers between devices with their start and end apart: 4, of which 2 were waited for; matrix products, arithmetic and copies ran while one was open for 10% of the time, Pallas kernels for 0%

commit v1 on v0

v1 whole, which is shorter than its diff:
```python
import jax
import jax.numpy as jnp
from jax import lax
from jax.sharding import PartitionSpec as P

eps_norm = 1e-06


def rms_scale(values, gain):
    mean_sq = jnp.mean(values * values, axis=-1, keepdims=True)
    return values * lax.rsqrt(mean_sq + eps_norm) * gain.astype(jnp.float32)


def on_device(
    attended,
    residual,
    new_kv,
    kv_pool,
    page_table,
    out_weight,
    router,
    attn_gain,
    ffn_gain,
    routes,
    replica_pick,
    lengths,
    slot_expert,
    slot_capacity,
    slot_in,
    slot_out,
):
    rows_dev, row_width = attended.shape
    experts_all = router.shape[1]
    slots_all = slot_expert.shape[0]
    top_count = routes.shape[1]
    holders = lax.axis_size("expert")
    slots_dev = slots_all // holders
    hidden_units = slot_out.shape[2]
    capacity = (rows_dev * top_count * 5 // (4 * slots_all) + 7) // 8 * 8
    bits = [1 << level for level in range(holders.bit_length() - 1)]

    side = -(-(experts_all + 2) // 128) * 128
    packed = jnp.concatenate(
        [
            out_weight,
            router,
            attn_gain[:, None],
            ffn_gain[:, None],
            jnp.zeros((out_weight.shape[0], side - experts_all - 2), jnp.bfloat16),
        ],
        axis=1,
    )
    packed_full = lax.all_gather(packed, ("dp", "expert"), axis=0, tiled=True)
    w_in = lax.all_gather(slot_in, "dp", axis=1, tiled=True)
    w_out = lax.all_gather(slot_out, "dp", axis=1, tiled=True)

    page_rows = kv_pool.shape[1]
    new_pages = new_kv.reshape(rows_dev // page_rows, page_rows, new_kv.shape[1])
    page_iota = lax.broadcasted_iota(jnp.int32, (kv_pool.shape[0], 1, 1), 0)
    pool_out = kv_pool
    for page in range(rows_dev // page_rows):
        pool_out = jnp.where(page_iota == page_table[page], new_pages[page][None], pool_out)

    same = slot_expert[:, None] == slot_expert[None, :]
    slot_before = (
        lax.broadcasted_iota(jnp.int32, (slots_all, slots_all), 0)
        < lax.broadcasted_iota(jnp.int32, (slots_all, slots_all), 1)
    )
    slot_copies = jnp.sum(same.astype(jnp.int32), axis=0)
    rank = jnp.sum((same & slot_before).astype(jnp.int32), axis=0)
    live_end = jnp.sum(lengths[:-1])
    row_first = lax.axis_index(("dp", "expert")) * rows_dev
    row_ids = row_first + lax.broadcasted_iota(jnp.int32, (rows_dev, 1), 0)
    live = row_ids < live_end
    chosen = jnp.zeros((rows_dev, slots_all), jnp.bool_)
    routed = jnp.zeros((rows_dev, experts_all), jnp.bool_)
    expert_iota = lax.broadcasted_iota(jnp.int32, (1, experts_all), 1)
    for k in range(top_count):
        route, pick = routes[:, k : k + 1], replica_pick[:, k : k + 1]
        chosen |= (route == slot_expert[None, :]) & (pick % slot_copies[None, :] == rank[None, :])
        routed |= route == expert_iota
    chosen &= live
    earlier = (
        lax.broadcasted_iota(jnp.int32, (rows_dev, rows_dev), 1)
        < lax.broadcasted_iota(jnp.int32, (rows_dev, rows_dev), 0)
    ).astype(jnp.bfloat16)
    position = jnp.dot(
        earlier, chosen.astype(jnp.bfloat16), preferred_element_type=jnp.float32
    )
    kept = chosen & (position < slot_capacity[None, :].astype(jnp.float32))
    place = jnp.where(kept, position, -1.0).astype(jnp.bfloat16)

    proj = jnp.dot(
        attended, packed_full[:, :row_width], preferred_element_type=jnp.float32
    )
    gain_first = packed_full[:, row_width + experts_all]
    gain_second = packed_full[:, row_width + experts_all + 1]
    router_full = packed_full[:, row_width : row_width + experts_all]
    hidden = (residual.astype(jnp.float32) + proj).astype(jnp.bfloat16)
    normed = rms_scale(hidden.astype(jnp.float32), gain_first).astype(jnp.bfloat16)
    logits = jnp.dot(normed, router_full, preferred_element_type=jnp.float32)
    raised = jnp.where(routed, jnp.exp(logits), 0.0)
    gates = raised / jnp.sum(raised, axis=1, keepdims=True)
    spread = (
        slot_expert[None, :] == lax.broadcasted_iota(jnp.int32, (experts_all, 1), 0)
    ).astype(jnp.float32)
    gate = jnp.where(kept, jnp.dot(gates, spread, precision=lax.Precision.HIGHEST), 0.0)
    gate_high = lax.reduce_precision(gate, 8, 7)
    gate_low = gate - gate_high

    meta = -(-3 * slots_all // 128) * 128
    table = jnp.concatenate(
        [
            place,
            gate_high.astype(jnp.bfloat16),
            gate_low.astype(jnp.bfloat16),
            jnp.zeros((rows_dev, meta - 3 * slots_all), jnp.bfloat16),
        ],
        axis=1,
    )
    blocks = {0: jnp.concatenate([normed, table], axis=1)}
    for bit in reversed(bits):
        pairs = [(i, i ^ bit) for i in range(holders)]
        for key in sorted(blocks):
            blocks[key ^ bit] = lax.ppermute(blocks[key], "expert", pairs)
    arrived = jnp.stack([blocks[key] for key in range(holders)])

    me = lax.axis_index("expert")
    tables = arrived[:, :, row_width : row_width + 3 * slots_all].reshape(
        holders, rows_dev, 3, slots_all
    )
    mine = lax.dynamic_slice_in_dim(tables, me * slots_dev, slots_dev, axis=3)
    mine = jnp.transpose(mine, (2, 0, 3, 1)).astype(jnp.float32)
    gate_rows = mine[1] + mine[2]
    spots = lax.broadcasted_iota(jnp.int32, (1, 1, capacity, 1), 2).astype(jnp.float32)
    hot = mine[0][:, :, None, :] == spots
    hot_low = hot.astype(jnp.bfloat16)
    slot_gate = jnp.sum(jnp.where(hot, gate_rows[:, :, None, :], 0.0), axis=3)

    rows_in = jnp.einsum(
        "hscr,hrd->hscd", hot_low, arrived[:, :, :row_width], preferred_element_type=jnp.float32
    ).astype(jnp.bfloat16)
    both = jnp.einsum("hscd,sdf->hscf", rows_in, w_in, preferred_element_type=jnp.float32)
    inner = (jax.nn.silu(both[..., :hidden_units]) * both[..., hidden_units:]).astype(jnp.bfloat16)
    result = jnp.einsum("hscf,sdf->hscd", inner, w_out, preferred_element_type=jnp.float32)
    scaled = (result * slot_gate[..., None]).astype(jnp.bfloat16)
    partial = jnp.einsum(
        "hscr,hscd->hrd", hot_low, scaled, preferred_element_type=jnp.float32
    ).astype(jnp.bfloat16)

    sums = {key: partial[key] for key in range(holders)}
    for bit in bits:
        pairs = [(i, i ^ bit) for i in range(holders)]
        for key in sorted(sums):
            if key & bit:
                came = lax.ppermute(sums.pop(key), "expert", pairs)
                joined = sums[key ^ bit].astype(jnp.float32) + came.astype(jnp.float32)
                last = bit == bits[-1]
                sums[key ^ bit] = joined if last else joined.astype(jnp.bfloat16)
    mixed = sums[0].astype(jnp.float32)
    total = hidden.astype(jnp.float32) + mixed
    residual_out = total.astype(jnp.bfloat16)
    next_normed = rms_scale(total, gain_second).astype(jnp.bfloat16)
    return (residual_out, next_normed, pool_out)


def solution(mesh):
    in_specs = (
        P(("dp", "expert"), None),
        P(("dp", "expert"), None),
        P(("dp", "expert"), None),
        P(("dp", "expert"), None, None),
        P(("dp", "expert")),
        P(("dp", "expert"), None),
        P(("dp", "expert"), None),
        P(("dp", "expert")),
        P(("dp", "expert")),
        P(("dp", "expert"), None),
        P(("dp", "expert"), None),
        P(),
        P(),
        P(),
        P("expert", "dp", None),
        P("expert", "dp", None),
    )
    out_specs = (
        P(("dp", "expert"), None),
        P(("dp", "expert"), None),
        P(("dp", "expert"), None, None),
    )
    return jax.shard_map(
        on_device, mesh=mesh, in_specs=in_specs, out_specs=out_specs, check_vma=False
    )
```

time: 475 us -> 342 us (0.72)
  blocking collectives: 314 us -> 0 us
  waiting for transfers between devices: 58.7 us -> 255 us
  local copies, waits for them, and re-layouts: 27.8 us -> 8.61 us
  other arithmetic: 25.3 us -> 6.34 us
  matrix products: 27.9 us -> 40.3 us
  starting transfers between devices: 5.77 us -> 16.3 us
    all_gather x1 -> x0, blocking collectives: 162 us -> none  [on_device(): router_piece = lax.all_gather(router, ('dp', 'expert'), axis=0, tiled=True)]
    all_to_all x1 -> x0, blocking collectives: 110 us -> none  [on_device(): lax.all_to_all(outgoing, 'expert', split_axis=0, concat_axis=0, tiled=True)]
    all_gather x3, waiting for transfers between devices: 56.7 us -> 166 us  [the longest x1 64.5 us: on_device(): packed_full = lax.all_gather(packed, ('dp', 'expert'), axis=0, tiled=True)]
    ppermute x0 -> x14, waiting for transfers between devices: none -> 87.9 us  [the longest x7 46.4 us: on_device(): blocks[key ^ bit] = lax.ppermute(blocks[key], 'expert', pairs)]
    unnamed x1 -> x0, blocking collectives: 42.6 us -> none
    ppermute x0 -> x14, starting transfers between devices: none -> 16.2 us  [the longest x7 8.53 us: on_device(): came = lax.ppermute(sums.pop(key), 'expert', pairs)]
    another operation x5 -> x0, other arithmetic: 14.6 us -> none
    dot_general x2 -> x5, matrix products: 17.3 us -> 28.3 us  [the longest x1 14.3 us: on_device(): jnp.einsum('hscd,sdf->hscf', rows_in, w_in, preferred_element_type=jnp.fl...]
  transfers between devices with their start and end apart: 4 -> 17, of which waited for: 2 -> 13; matrix products, arithmetic and copies ran while one was open for 10% -> 9% of each run, Pallas kernels for 0% -> 0%
where the time goes in v1:
time: 342 us
  waiting for transfers between devices  255 us (75%)
  matrix products  40.3 us (12%)
  starting transfers between devices  16.3 us (5%)
  between operations  14.8 us (4%)
  local copies, waits for them, and re-layouts  8.61 us (3%)
  other arithmetic  6.34 us (2%)
    all_gather x1, waiting for transfers between devices, on_device(): packed_full = lax.all_gather(packed, ('dp', 'expert'), axis=0, tiled=True)  64.5 us
    all_gather x1, waiting for transfers between devices, on_device(): w_out = lax.all_gather(slot_out, 'dp', axis=1, tiled=True)  51.6 us
    all_gather x1, waiting for transfers between devices, on_device(): w_in = lax.all_gather(slot_in, 'dp', axis=1, tiled=True)  50 us
    ppermute x7, waiting for transfers between devices, on_device(): blocks[key ^ bit] = lax.ppermute(blocks[key], 'expert', pairs)  46.4 us
    ppermute x7, waiting for transfers between devices, on_device(): came = lax.ppermute(sums.pop(key), 'expert', pairs)  41.6 us
    dot_general x1, matrix products, on_device(): jnp.einsum('hscd,sdf->hscf', rows_in, w_in, preferred_element_type=jnp.fl...  14.3 us
    dot_general x1, matrix products, on_device(): jnp.einsum('hscf,sdf->hscd', inner, w_out, preferred_element_type=jnp.flo...  10.3 us
    ppermute x7, starting transfers between devices, on_device(): came = lax.ppermute(sums.pop(key), 'expert', pairs)  8.53 us
  transfers between devices with their start and end apart: 17, of which 13 were waited for; matrix products, arithmetic and copies ran while one was open for 9% of the time, Pallas kernels for 0%

profile of v1, /device:TPU:0, one launch (start us, length us, event | category | flops | bytes accessed | tf_op | source)
XLA Modules:
  0.0 341.8 jit_solution(943933566831437832)
XLA Ops:
  7.2 0.8 copy.34
  8.1 0.8 copy.35
  8.8 0.8 copy.36
  9.6 1.7 concatenate.6
  11.4 0.7 all-gather.6.cloned.1.call-update
  12.1 0.7 all-gather.8.cloned.1.call-update
  13.1 0.6 slice_reduce_fusion
  13.8 0.7 add_compare_fusion
  14.6 64.5 %all-gather.4.cloned.1.call-done = bf16[1536,1664]{1,0:T(8,128)(2,1)} async-done(((bf16[48,1664]{1,0:T(8,128)(2,1)}), bf16[1536,1664]{1,0:T(8,128)(2,1)}) %all-gather.4.cloned.1.call-update) | async-done | bytes 5111824 | tf_op jit(solution)/shard_map/all_gather | solution.py:53
  79.1 1.7 convert_reduce_fusion
  80.8 3.8 %multiply_reduce_fusion.1 = (f32[128]{0:T(128)S(1)}, f32[128,1536]{0,1:T(8,128)S(1)}) fusion(bf16[128,1536]{1,0:T(8,128)(2,1)S(1)} %copy-done, bf16[1536,1664]{1,0:T(8,128)(2,1)} %all-gather.4.cloned.1.call-done, bf16[128,1536]{0,1:T(8,128)(2,1)S(1)} %copy.33), kind=kOutput, calls=%fused_computation.41 | convolution fusion | flops 605159296 | bytes 6291968 | tf_op jit(solution)/shard_map/dot_general | solution.py:93
  84.9 3.8 %constant_dynamic-update-slice_fusion.3 = (bf16[128,1792]{0,1:T(8,128)(2,1)S(1)}, f32[128,48]{0,1:T(8,128)S(1)}) fusion(bf16[128,1792]{0,1:T(8,128)(2,1)S(1)} %constant_dynamic-update-slice_fusion.4, f32[48]{0:T(128)S(1)} %convert_element_type.168, pred[128]{0:T(512)(128)(4,1)S(1)} %add_compare_fusion, s32[128]{0:T(128)S(1)} %get-tuple-element.43, ...), kind=kOutput, calls=%fused_computation.109 | convolution fusion | flops 2695168 | bytes 58880 | tf_op jit(solution)/shard_map/dot_general | solution.py:87
  88.7 1.6 fusion.97
  90.4 2.0 constant_dynamic-update-slice_fusion.2
  92.4 1.5 collective-permute-start
  93.9 1.9 collective-permute-start.1
  95.8 0.8 collective-permute-start.3
  96.7 22.1 %collective-permute-done.3 = bf16[128,1792]{0,1:T(8,128)(2,1)S(1)} collective-permute-done((bf16[128,1792]{0,1:T(8,128)(2,1)S(1)}, bf16[128,1792]{0,1:T(8,128)(2,1)S(1)}, u32[]{:S(2)}, u32[]{:S(2)}) %collective-permute-start.3) | collective-permute-done | bytes 458784 | tf_op jit(solution)/shard_map/ppermute | solution.py:125
  118.7 0.5 collective-permute-start.4
  119.3 1.5 collective-permute-start.2
  120.9 7.7 %collective-permute-done.5 = bf16[128,1792]{0,1:T(8,128)(2,1)S(1)} collective-permute-done((bf16[128,1792]{0,1:T(8,128)(2,1)S(1)}, bf16[128,1792]{0,1:T(8,128)(2,1)S(1)}, u32[]{:S(2)}, u32[]{:S(2)}) %collective-permute-start.5) | collective-permute-done | bytes 458784 | tf_op jit(solution)/shard_map/ppermute | solution.py:125
  128.6 1.4 collective-permute-start.6
  129.9 12.0 %collective-permute-done.2 = bf16[128,1792]{0,1:T(8,128)(2,1)S(1)} collective-permute-done((bf16[128,1792]{0,1:T(8,128)(2,1)S(1)}, bf16[128,1792]{0,1:T(8,128)(2,1)S(1)}, u32[]{:S(2)}, u32[]{:S(2)}) %collective-permute-start.2) | collective-permute-done | bytes 458784 | tf_op jit(solution)/shard_map/ppermute | solution.py:125
  142.2 4.6 %collective-permute-done.6 = bf16[128,1792]{0,1:T(8,128)(2,1)S(1)} collective-permute-done((bf16[128,1792]{0,1:T(8,128)(2,1)S(1)}, bf16[128,1792]{0,1:T(8,128)(2,1)S(1)}, u32[]{:S(2)}, u32[]{:S(2)}) %collective-permute-start.6) | collective-permute-done | bytes 458784 | tf_op jit(solution)/shard_map/ppermute | solution.py:125
  147.0 1.8 copy-done.5
  148.8 0.3 select_reduce_fusion
  149.2 50.0 %all-gather.6.cloned.1.call-done = bf16[6,1536,1024]{2,1,0:T(8,128)(2,1)} async-done(((bf16[6,384,1024]{2,1,0:T(8,128)(2,1)}), bf16[6,1536,1024]{2,1,0:T(8,128)(2,1)}) %all-gather.6.cloned.1.call-update) | async-done | bytes 18874384 | tf_op jit(solution)/shard_map/all_gather | solution.py:54
  199.2 14.3 %fusion.12 = f32[8,6,32,1024]{3,2,0,1:T(8,128)} fusion(bf16[6,1536,1024]{2,1,0:T(8,128)(2,1)} %all-gather.6.cloned.1.call-done, bf16[8,128,1792]{1,2,0:T(8,128)(2,1)} %copy-done.5, f32[8,6,128]{2,1,0:T(8,128)S(1)} %get-tuple-element.27, f32[32]{0:T(128)S(1)} %iota_convert_fusion), kind=kOutput, calls=%fused_computation.14 | convolution fusion | flops 5438373888 | bytes 28336256 | tf_op jit(solution)/shard_map/hscd,sdf->hscf/dot_general | solution.py:143
  213.5 51.6 %all-gather.8.cloned.1.call-done = bf16[6,1536,512]{2,1,0:T(8,128)(2,1)} async-done(((bf16[6,384,512]{2,1,0:T(8,128)(2,1)}), bf16[6,1536,512]{2,1,0:T(8,128)(2,1)}) %all-gather.8.cloned.1.call-update) | async-done | bytes 9437200 | tf_op jit(solution)/shard_map/all_gather | solution.py:55
  265.1 10.3 %fusion.2 = bf16[8,6,32,1536]{3,2,1,0:T(8,128)(2,1)} fusion(bf16[6,1536,512]{2,1,0:T(8,128)(2,1)} %all-gather.8.cloned.1.call-done, f32[8,6,32]{2,1,0:T(8,128)S(1)} %select_reduce_fusion, f32[8,6,32,1024]{3,2,0,1:T(8,128)} %fusion.12), kind=kOutput, calls=%fused_computation.3 | convolution fusion | flops 2425356288 | bytes 20453376 | tf_op jit(solution)/shard_map/hscf,sdf->hscd/dot_general | solution.py:145
  275.4 4.5 %bitcast_convert_fusion = bf16[8,128,1536]{1,2,0:T(8,128)(2,1)S(1)} fusion(bf16[8,6,32,1536]{3,2,1,0:T(8,128)(2,1)} %fusion.2, f32[8,6,128]{2,1,0:T(8,128)S(1)} %get-tuple-element.27, f32[32]{0:T(128)S(1)} %iota_convert_fusion), kind=kOutput, calls=%fused_computation.6 | convolution fusion | flops 605749248 | bytes 7889024 | tf_op jit(solution)/shard_map/hscr,hscd->hrd/dot_general | solution.py:147
  280.1 1.5 collective-permute-start.11
  281.6 0.6 collective-permute-start.8
  282.2 1.5 collective-permute-start.10
  283.6 8.4 %collective-permute-done.11 = bf16[128,1536]{0,1:T(8,128)(2,1)S(1)} collective-permute-done((bf16[128,1536]{0,1:T(8,128)(2,1)S(1)}, bf16[128,1536]{0,1:T(8,128)(2,1)S(1)}, u32[]{:S(2)}, u32[]{:S(2)}) %collective-permute-start.11) | collective-permute-done | bytes 393248 | tf_op jit(solution)/shard_map/ppermute | solution.py:156
  292.1 8.4 %collective-permute-done.8 = bf16[128,1536]{0,1:T(8,128)(2,1)S(1)} collective-permute-done((bf16[128,1536]{0,1:T(8,128)(2,1)S(1)}, bf16[128,1536]{0,1:T(8,128)(2,1)S(1)}, u32[]{:S(2)}, u32[]{:S(2)}) %collective-permute-start.8) | collective-permute-done | bytes 393248 | tf_op jit(solution)/shard_map/ppermute | solution.py:156
  300.7 1.6 collective-permute-start.12
  302.9 1.5 collective-permute-start.7
  304.5 0.5 collective-permute-start.9
  305.0 3.9 %collective-permute-done.10 = bf16[128,1536]{0,1:T(8,128)(2,1)S(1)} collective-permute-done((bf16[128,1536]{0,1:T(8,128)(2,1)S(1)}, bf16[128,1536]{0,1:T(8,128)(2,1)S(1)}, u32[]{:S(2)}, u32[]{:S(2)}) %collective-permute-start.10) | collective-permute-done | bytes 393248 | tf_op jit(solution)/shard_map/ppermute | solution.py:156
  308.9 8.1 %collective-permute-done.12 = bf16[128,1536]{0,1:T(8,128)(2,1)S(1)} collective-permute-done((bf16[128,1536]{0,1:T(8,128)(2,1)S(1)}, bf16[128,1536]{0,1:T(8,128)(2,1)S(1)}, u32[]{:S(2)}, u32[]{:S(2)}) %collective-permute-start.12) | collective-permute-done | bytes 393248 | tf_op jit(solution)/shard_map/ppermute | solution.py:156
  317.2 1.3 collective-permute-start.13
  318.6 1.6 broadcast_select_fusion
  320.1 3.9 %collective-permute-done.9 = bf16[128,1536]{0,1:T(8,128)(2,1)S(1)} collective-permute-done((bf16[128,1536]{0,1:T(8,128)(2,1)S(1)}, bf16[128,1536]{0,1:T(8,128)(2,1)S(1)}, u32[]{:S(2)}, u32[]{:S(2)}) %collective-permute-start.9) | collective-permute-done | bytes 393248 | tf_op jit(solution)/shard_map/ppermute | solution.py:156
  324.0 8.8 %collective-permute-done.13 = bf16[128,1536]{0,1:T(8,128)(2,1)S(1)} collective-permute-done((bf16[128,1536]{0,1:T(8,128)(2,1)S(1)}, bf16[128,1536]{0,1:T(8,128)(2,1)S(1)}, u32[]{:S(2)}, u32[]{:S(2)}) %collective-permute-start.13) | collective-permute-done | bytes 393248 | tf_op jit(solution)/shard_map/ppermute | solution.py:156
  333.1 0.3 multiply_convert_fusion
  333.4 0.9 copy.41
  334.3 0.9 copy.42
  (59 shorter events, 2.2 us)
Async XLA Ops:
  7.2 73.6 %copy-start = (bf16[128,1536]{1,0:T(8,128)(2,1)S(1)}, bf16[128,1536]{1,0:T(8,128)(2,1)}, u32[]{:S(2)}) copy-start(bf16[128,1536]{1,0:T(8,128)(2,1)} %param.18) | copy-start | bytes 1179652
  7.2 71.9 %all-gather.4.cloned.1.call-start = ((), (), s32[]{:S(2)}) async-start(), calls=%async_computation | async-start | bytes 5271552 | tf_op jit(solution)/shard_map/all_gather | solution.py:53
  11.2 1.6 copy-start.3
  11.3 1.8 copy-start.9
  11.3 1.9 copy-start.10
  11.3 3.1 copy-start.8
  11.3 3.3 copy-start.6
  11.3 3.3 copy-start.7
  11.3 187.9 %all-gather.6.cloned.1.call-start = ((), (), s32[]{:S(2)}) async-start(), calls=%async_computation.1 | async-start | bytes 23592960 | tf_op jit(solution)/shard_map/all_gather | solution.py:54
  12.1 253.0 %all-gather.8.cloned.1.call-start = ((), (), s32[]{:S(2)}) async-start(), calls=%async_computation.2 | async-start | bytes 11796480 | tf_op jit(solution)/shard_map/all_gather | solution.py:55
  92.4 28.4 %collective-permute-start = (bf16[128,1792]{0,1:T(8,128)(2,1)S(1)}, bf16[128,1792]{0,1:T(8,128)(2,1)S(1)}, u32[]{:S(2)}, u32[]{:S(2)}) collective-permute-start(bf16[128,1792]{0,1:T(8,128)(2,1)S(1)} %constant_dynamic-update-slice_fusion), channel_id=1, source_target_pairs={{0,1},{1,0},{2,3},{3,2},{4,5},{5,4},{6,7},{7,6},{8,9},{9,8},{10,11... | collective-permute-start | bytes 1376264 | tf_op jit(solution)/shard_map/ppermute | solution.py:125
  93.9 25.4 %collective-permute-start.1 = (bf16[128,1792]{0,1:T(8,128)(2,1)S(1)}, bf16[128,1792]{0,1:T(8,128)(2,1)S(1)}, u32[]{:S(2)}, u32[]{:S(2)}) collective-permute-start(bf16[128,1792]{0,1:T(8,128)(2,1)S(1)} %constant_dynamic-update-slice_fusion), channel_id=1, source_target_pairs={{0,2},{1,3},{2,0},{3,1},{4,6},{5,7},{6,4},{7,5},{8,10},{9,11},{10,... | collective-permute-start | bytes 1376264 | tf_op jit(solution)/shard_map/ppermute | solution.py:125
  95.8 22.9 %collective-permute-start.3 = (bf16[128,1792]{0,1:T(8,128)(2,1)S(1)}, bf16[128,1792]{0,1:T(8,128)(2,1)S(1)}, u32[]{:S(2)}, u32[]{:S(2)}) collective-permute-start(bf16[128,1792]{0,1:T(8,128)(2,1)S(1)} %constant_dynamic-update-slice_fusion), channel_id=1, source_target_pairs={{0,4},{1,5},{2,6},{3,7},{4,0},{5,1},{6,2},{7,3},{8,12},{9,13},{10,... | collective-permute-start | bytes 1376264 | tf_op jit(solution)/shard_map/ppermute | solution.py:125
  118.7 23.3 %collective-permute-start.4 = (bf16[128,1792]{0,1:T(8,128)(2,1)S(1)}, bf16[128,1792]{0,1:T(8,128)(2,1)S(1)}, u32[]{:S(2)}, u32[]{:S(2)}) collective-permute-start(bf16[128,1792]{0,1:T(8,128)(2,1)S(1)} %collective-permute-done.3), channel_id=1, source_target_pairs={{0,1},{1,0},{2,3},{3,2},{4,5},{5,4},{6,7},{7,6},{8,9},{9,8},{10,11... | collective-permute-start | bytes 1376264 | tf_op jit(solution)/shard_map/ppermute | solution.py:125
  119.3 9.3 %collective-permute-start.5 = (bf16[128,1792]{0,1:T(8,128)(2,1)S(1)}, bf16[128,1792]{0,1:T(8,128)(2,1)S(1)}, u32[]{:S(2)}, u32[]{:S(2)}) collective-permute-start(bf16[128,1792]{0,1:T(8,128)(2,1)S(1)} %collective-permute-done.3), channel_id=1, source_target_pairs={{0,2},{1,3},{2,0},{3,1},{4,6},{5,7},{6,4},{7,5},{8,10},{9,11},{10,... | collective-permute-start | bytes 1376264 | tf_op jit(solution)/shard_map/ppermute | solution.py:125
  119.3 22.6 %collective-permute-start.2 = (bf16[128,1792]{0,1:T(8,128)(2,1)S(1)}, bf16[128,1792]{0,1:T(8,128)(2,1)S(1)}, u32[]{:S(2)}, u32[]{:S(2)}) collective-permute-start(bf16[128,1792]{0,1:T(8,128)(2,1)S(1)} %collective-permute-done.1), channel_id=1, source_target_pairs={{0,1},{1,0},{2,3},{3,2},{4,5},{5,4},{6,7},{7,6},{8,9},{9,8},{10,11... | collective-permute-start | bytes 1376264 | tf_op jit(solution)/shard_map/ppermute | solution.py:125
  128.6 18.3 %collective-permute-start.6 = (bf16[128,1792]{0,1:T(8,128)(2,1)S(1)}, bf16[128,1792]{0,1:T(8,128)(2,1)S(1)}, u32[]{:S(2)}, u32[]{:S(2)}) collective-permute-start(bf16[128,1792]{0,1:T(8,128)(2,1)S(1)} %collective-permute-done.5), channel_id=1, source_target_pairs={{0,1},{1,0},{2,3},{3,2},{4,5},{5,4},{6,7},{7,6},{8,9},{9,8},{10,11... | collective-permute-start | bytes 1376264 | tf_op jit(solution)/shard_map/ppermute | solution.py:125
  146.9 1.9 copy-start.5
  279.9 38.6 %copy-start.2 = (bf16[8,128,1024]{2,1,0:T(8,128)(2,1)S(1)}, bf16[8,128,1024]{2,1,0:T(8,128)(2,1)}, u32[]{:S(2)}) copy-start(bf16[8,128,1024]{2,1,0:T(8,128)(2,1)} %param.21) | copy-start | bytes 6291460
  279.9 38.6 %copy-start.4 = (bf16[128,1024]{1,0:T(8,128)(2,1)S(1)}, bf16[128,1024]{1,0:T(8,128)(2,1)}, u32[]{:S(2)}) copy-start(bf16[128,1024]{1,0:T(8,128)(2,1)} %param.20) | copy-start | bytes 786436
  280.1 12.0 %collective-permute-start.11 = (bf16[128,1536]{0,1:T(8,128)(2,1)S(1)}, bf16[128,1536]{0,1:T(8,128)(2,1)S(1)}, u32[]{:S(2)}, u32[]{:S(2)}) collective-permute-start(bf16[128,1536]{0,1:T(8,128)(2,1)S(1)} %get-tuple-element.20), channel_id=1, source_target_pairs={{0,1},{1,0},{2,3},{3,2},{4,5},{5,4},{6,7},{7,6},{8,9},{9,8},{10,11... | collective-permute-start | bytes 1179656 | tf_op jit(solution)/shard_map/ppermute | solution.py:156
  281.6 18.9 %collective-permute-start.8 = (bf16[128,1536]{0,1:T(8,128)(2,1)S(1)}, bf16[128,1536]{0,1:T(8,128)(2,1)S(1)}, u32[]{:S(2)}, u32[]{:S(2)}) collective-permute-start(bf16[128,1536]{0,1:T(8,128)(2,1)S(1)} %get-tuple-element.22), channel_id=1, source_target_pairs={{0,1},{1,0},{2,3},{3,2},{4,5},{5,4},{6,7},{7,6},{8,9},{9,8},{10,11... | collective-permute-start | bytes 1179656 | tf_op jit(solution)/shard_map/ppermute | solution.py:156
  282.2 26.8 %collective-permute-start.10 = (bf16[128,1536]{0,1:T(8,128)(2,1)S(1)}, bf16[128,1536]{0,1:T(8,128)(2,1)S(1)}, u32[]{:S(2)}, u32[]{:S(2)}) collective-permute-start(bf16[128,1536]{0,1:T(8,128)(2,1)S(1)} %get-tuple-element.21), channel_id=1, source_target_pairs={{0,1},{1,0},{2,3},{3,2},{4,5},{5,4},{6,7},{7,6},{8,9},{9,8},{10,11... | collective-permute-start | bytes 1179656 | tf_op jit(solution)/shard_map/ppermute | solution.py:156
  300.7 16.3 %collective-permute-start.12 = (bf16[128,1536]{0,1:T(8,128)(2,1)S(1)}, bf16[128,1536]{0,1:T(8,128)(2,1)S(1)}, u32[]{:S(2)}, u32[]{:S(2)}) collective-permute-start(bf16[128,1536]{0,1:T(8,128)(2,1)S(1)} %get-tuple-element.24), channel_id=1, source_target_pairs={{0,2},{1,3},{2,0},{3,1},{4,6},{5,7},{6,4},{7,5},{8,10},{9,11},{10,... | collective-permute-start | bytes 1179656 | tf_op jit(solution)/shard_map/ppermute | solution.py:156
  302.9 17.2 %collective-permute-start.7 = (bf16[128,1536]{0,1:T(8,128)(2,1)S(1)}, bf16[128,1536]{0,1:T(8,128)(2,1)S(1)}, u32[]{:S(2)}, u32[]{:S(2)}) collective-permute-start(bf16[128,1536]{0,1:T(8,128)(2,1)S(1)} %get-tuple-element.19), channel_id=1, source_target_pairs={{0,1},{1,0},{2,3},{3,2},{4,5},{5,4},{6,7},{7,6},{8,9},{9,8},{10,11... | collective-permute-start | bytes 1179656 | tf_op jit(solution)/shard_map/ppermute | solution.py:156
  304.5 19.6 %collective-permute-start.9 = (bf16[128,1536]{0,1:T(8,128)(2,1)S(1)}, bf16[128,1536]{0,1:T(8,128)(2,1)S(1)}, u32[]{:S(2)}, u32[]{:S(2)}) collective-permute-start(bf16[128,1536]{0,1:T(8,128)(2,1)S(1)} %get-tuple-element.23), channel_id=1, source_target_pairs={{0,2},{1,3},{2,0},{3,1},{4,6},{5,7},{6,4},{7,5},{8,10},{9,11},{10,... | collective-permute-start | bytes 1179656 | tf_op jit(solution)/shard_map/ppermute | solution.py:156
  317.2 15.6 %collective-permute-start.13 = (bf16[128,1536]{0,1:T(8,128)(2,1)S(1)}, bf16[128,1536]{0,1:T(8,128)(2,1)S(1)}, u32[]{:S(2)}, u32[]{:S(2)}) collective-permute-start(bf16[128,1536]{0,1:T(8,128)(2,1)S(1)} %add_convert_fusion), channel_id=1, source_target_pairs={{0,4},{1,5},{2,6},{3,7},{4,0},{5,1},{6,2},{7,3},{8,12},{9,13},{10,... | collective-permute-start | bytes 1179656 | tf_op jit(solution)/shard_map/ppermute | solution.py:156
  318.5 16.7 %copy-start.1 = (bf16[128,1536]{1,0:T(8,128)(2,1)S(1)}, bf16[128,1536]{1,0:T(8,128)(2,1)}, u32[]{:S(2)}) copy-start(bf16[128,1536]{1,0:T(8,128)(2,1)} %param.18) | copy-start | bytes 1179652
Sparse Core Ops, SparseCore 0:
  11.5 67.5 all-gather.3
  80.6 118.5 all-gather.5
  200.8 64.2 all-gather.7

commit v2 on v1

--- a/solution.py
+++ b/solution.py
@@ -9,6 +9,33 @@
 def rms_scale(values, gain):
     mean_sq = jnp.mean(values * values, axis=-1, keepdims=True)
     return values * lax.rsqrt(mean_sq + eps_norm) * gain.astype(jnp.float32)
+
+
+def spread_by_doubling(block, bits):
+    dp_bits = [1 << level for level in range(lax.axis_size("dp").bit_length() - 1)]
+    outer = len(dp_bits) - 1 if dp_bits else 0
+    steps = [("dp", bit, at) for at, bit in enumerate(reversed(dp_bits[1:]))]
+    steps += [("expert", bit, outer + at) for at, bit in enumerate(reversed(bits))]
+    steps += [("dp", bit, outer) for bit in dp_bits[:1]]
+    held = block
+    for name, bit, at in steps:
+        pairs = [(i, i ^ bit) for i in range(lax.axis_size(name))]
+        came = lax.ppermute(held, name, pairs)
+        upper = (lax.axis_index(name) & bit) != 0
+        held = jnp.stack([jnp.where(upper, came, held), jnp.where(upper, held, came)], axis=at)
+    return held.reshape(-1, block.shape[1])
+
+
+def halve_sums(sums, bit):
+    pairs = [(i, i ^ bit) for i in range(lax.axis_size("expert"))]
+    kept_sums = {}
+    for key in sorted(sums):
+        if key & bit:
+            came = lax.ppermute(sums[key], "expert", pairs)
+            joined = sums[key ^ bit].astype(jnp.float32) + came.astype(jnp.float32)
+            last = len(sums) == 2
+            kept_sums[key ^ bit] = joined if last else joined.astype(jnp.bfloat16)
+    return kept_sums
 
 
 def on_device(
@@ -50,9 +77,12 @@
         ],
         axis=1,
     )
-    packed_full = lax.all_gather(packed, ("dp", "expert"), axis=0, tiled=True)
+    packed_full = spread_by_doubling(packed, bits)
     w_in = lax.all_gather(slot_in, "dp", axis=1, tiled=True)
-    w_out = lax.all_gather(slot_out, "dp", axis=1, tiled=True)
+    features = slot_out.shape[1]
+    first = min(features, -(-features // 256) * 128)
+    cuts = [(0, first), (first, features)] if first < features else [(0, features)]
+    w_out = [lax.all_gather(slot_out[:, lo:hi], "dp", axis=1, tiled=True) for lo, hi in cuts]
 
     page_rows = kv_pool.shape[1]
     new_pages = new_kv.reshape(rows_dev // page_rows, page_rows, new_kv.shape[1])
@@ -142,22 +172,23 @@
     ).astype(jnp.bfloat16)
     both = jnp.einsum("hscd,sdf->hscf", rows_in, w_in, preferred_element_type=jnp.float32)
     inner = (jax.nn.silu(both[..., :hidden_units]) * both[..., hidden_units:]).astype(jnp.bfloat16)
-    result = jnp.einsum("hscf,sdf->hscd", inner, w_out, preferred_element_type=jnp.float32)
-    scaled = (result * slot_gate[..., None]).astype(jnp.bfloat16)
-    partial = jnp.einsum(
-        "hscr,hscd->hrd", hot_low, scaled, preferred_element_type=jnp.float32
-    ).astype(jnp.bfloat16)
-
-    sums = {key: partial[key] for key in range(holders)}
-    for bit in bits:
-        pairs = [(i, i ^ bit) for i in range(holders)]
-        for key in sorted(sums):
-            if key & bit:
-                came = lax.ppermute(sums.pop(key), "expert", pairs)
-                joined = sums[key ^ bit].astype(jnp.float32) + came.astype(jnp.float32)
-                last = bit == bits[-1]
-                sums[key ^ bit] = joined if last else joined.astype(jnp.bfloat16)
-    mixed = sums[0].astype(jnp.float32)
+    trees = []
+    for part in w_out:
+        if trees and bits:
+            part = lax.optimization_barrier((trees[-1], part))[1]
+        result = jnp.einsum("hscf,sdf->hscd", inner, part, preferred_element_type=jnp.float32)
+        scaled = (result * slot_gate[..., None]).astype(jnp.bfloat16)
+        partial = jnp.einsum(
+            "hscr,hscd->hrd", hot_low, scaled, preferred_element_type=jnp.float32
+        ).astype(jnp.bfloat16)
+        sums = {key: partial[key] for key in range(holders)}
+        trees.append(halve_sums(sums, bits[0]) if bits else sums)
+    pieces = []
+    for sums in trees:
+        for bit in bits[1:]:
+            sums = halve_sums(sums, bit)
+        pieces.append(sums[0].astype(jnp.float32).reshape(rows_dev, lax.axis_size("dp"), -1))
+    mixed = jnp.concatenate(pieces, axis=2).reshape(rows_dev, row_width)
     total = hidden.astype(jnp.float32) + mixed
     residual_out = total.astype(jnp.bfloat16)
     next_normed = rms_scale(total, gain_second).astype(jnp.bfloat16)

time: 342 us -> 262 us (0.77)
  waiting for transfers between devices: 255 us -> 146 us
  starting transfers between devices: 16.3 us -> 37.7 us
  other arithmetic: 6.34 us -> 19.2 us
  matrix products: 40.3 us -> 31.8 us
  local copies, waits for them, and re-layouts: 8.61 us -> 12.3 us
    all_gather x2, waiting for transfers between devices: 116 us -> 5.61 us  [on_device(): lax.all_gather(slot_out[:, lo:hi], 'dp', axis=1, tiled=True)]
    ppermute x7 -> x19, waiting for transfers between devices: 41.6 us -> 101 us  [the longest x5 60.1 us: spread_by_doubling(): came = lax.ppermute(held, name, pairs)]
    all_gather x1, waiting for transfers between devices: 50 us -> 0.02 us  [on_device(): w_in = lax.all_gather(slot_in, 'dp', axis=1, tiled=True)]
    ppermute x7 -> x19, starting transfers between devices: 8.53 us -> 22.3 us  [the longest x14 14.3 us: halve_sums(): came = lax.ppermute(sums[key], 'expert', pairs)]
    ppermute x7, starting transfers between devices: 7.68 us -> 15.3 us  [on_device(): blocks[key ^ bit] = lax.ppermute(blocks[key], 'expert', pairs)]
    ppermute x7, waiting for transfers between devices: 46.4 us -> 39 us  [on_device(): blocks[key ^ bit] = lax.ppermute(blocks[key], 'expert', pairs)]
    another operation x0 -> x10, other arithmetic: none -> 7.03 us  [spread_by_doubling(): jnp.stack([jnp.where(upper, came, held), jnp.where(upper, held, came)], a...]
    convert_element_type x2 -> x5, other arithmetic: 0.36 us -> 6.23 us  [the longest x1 3.93 us: on_device(): (jax.nn.silu(both[..., :hidden_units]) * both[..., hidden_units:]).astype...]
  transfers between devices with their start and end apart: 17 -> 29, of which waited for: 13 -> 20; matrix products, arithmetic and copies ran while one was open for 9% -> 19% of each run, Pallas kernels for 0% -> 0%
where the time goes in v2:
time: 262 us
  waiting for transfers between devices  146 us (56%)
  starting transfers between devices  37.7 us (14%)
  matrix products  31.8 us (12%)
  other arithmetic  19.2 us (7%)
  between operations  15 us (6%)
  local copies, waits for them, and re-layouts  12.3 us (5%)
    ppermute x5, waiting for transfers between devices, spread_by_doubling(): came = lax.ppermute(held, name, pairs)  60.1 us
    ppermute x14, waiting for transfers between devices, halve_sums(): came = lax.ppermute(sums[key], 'expert', pairs)  40.6 us
    ppermute x7, waiting for transfers between devices, on_device(): blocks[key ^ bit] = lax.ppermute(blocks[key], 'expert', pairs)  39 us
    ppermute x7, starting transfers between devices, on_device(): blocks[key ^ bit] = lax.ppermute(blocks[key], 'expert', pairs)  15.3 us
    ppermute x14, starting transfers between devices, halve_sums(): came = lax.ppermute(sums[key], 'expert', pairs)  14.3 us
    dot_general x1, matrix products, on_device(): jnp.einsum('hscd,sdf->hscf', rows_in, w_in, preferred_element_type=jnp.fl...  14.1 us
    ppermute x5, starting transfers between devices, spread_by_doubling(): came = lax.ppermute(held, name, pairs)  7.98 us
    another operation x10, other arithmetic, spread_by_doubling(): jnp.stack([jnp.where(upper, came, held), jnp.where(upper, held, came)], a...  7.03 us
  transfers between devices with their start and end apart: 29, of which 20 were waited for; matrix products, arithmetic and copies ran while one was open for 19% of the time, Pallas kernels for 0%

profile of v2, /device:TPU:0, one launch (start us, length us, event | category | flops | bytes accessed | tf_op | source)
XLA Modules:
  0.0 261.9 jit_solution(2224206285716484280)
XLA Ops:
  10.7 3.0 %collective-permute-start = (bf16[48,1664]{1,0:T(8,128)(2,1)S(1)}, bf16[48,1664]{1,0:T(8,128)(2,1)S(1)}, u32[]{:S(2)}, u32[]{:S(2)}) collective-permute-start(bf16[48,1664]{1,0:T(8,128)(2,1)S(1)} %concatenate.9), channel_id=1, source_target_pairs={{0,16},{8,24},{16,0},{24,8},{1,17},{9,25},{17,1},{25,9},{2,18},{10... | collective-permute-start | bytes 479240 | tf_op jit(solution)/shard_map/ppermute | solution.py:23
  13.7 4.1 %collective-permute-done = bf16[48,1664]{1,0:T(8,128)(2,1)S(1)} collective-permute-done((bf16[48,1664]{1,0:T(8,128)(2,1)S(1)}, bf16[48,1664]{1,0:T(8,128)(2,1)S(1)}, u32[]{:S(2)}, u32[]{:S(2)}) %collective-permute-start) | collective-permute-done | bytes 159776 | tf_op jit(solution)/shard_map/ppermute | solution.py:23
  17.9 2.9 %collective-permute-start.1 = (bf16[2,48,1664]{2,1,0:T(8,128)(2,1)S(1)}, bf16[2,48,1664]{2,1,0:T(8,128)(2,1)S(1)}, u32[]{:S(2)}, u32[]{:S(2)}) collective-permute-start(bf16[2,48,1664]{2,1,0:T(8,128)(2,1)S(1)} %pad_maximum_fusion.5), channel_id=1, source_target_pairs={{0,4},{1,5},{2,6},{3,7},{4,0},{5,1},{6,2},{7,3},{8,12},{9,13},{10,... | collective-permute-start | bytes 958472 | tf_op jit(solution)/shard_map/ppermute | solution.py:23
  20.8 13.6 %collective-permute-done.1 = bf16[2,48,1664]{2,1,0:T(8,128)(2,1)S(1)} collective-permute-done((bf16[2,48,1664]{2,1,0:T(8,128)(2,1)S(1)}, bf16[2,48,1664]{2,1,0:T(8,128)(2,1)S(1)}, u32[]{:S(2)}, u32[]{:S(2)}) %collective-permute-start.1) | collective-permute-done | bytes 319520 | tf_op jit(solution)/shard_map/ppermute | solution.py:23
  35.2 14.7 %collective-permute-done.2 = bf16[2,2,48,1664]{3,2,1,0:T(8,128)(2,1)S(1)} collective-permute-done((bf16[2,2,48,1664]{3,2,1,0:T(8,128)(2,1)S(1)}, bf16[2,2,48,1664]{3,2,1,0:T(8,128)(2,1)S(1)}, u32[]{:S(2)}, u32[]{:S(2)}) %collective-permute-start.2) | collective-permute-done | bytes 639008 | tf_op jit(solution)/shard_map/ppermute | solution.py:23
  51.1 1.4 collective-permute-start.3
  52.5 27.0 %collective-permute-done.3 = bf16[2,2,2,48,1664]{4,3,2,1,0:T(8,128)(2,1)} collective-permute-done((bf16[2,2,2,48,1664]{4,3,2,1,0:T(8,128)(2,1)S(1)}, bf16[2,2,2,48,1664]{4,3,2,1,0:T(8,128)(2,1)}, u32[]{:S(2)}, u32[]{:S(2)}) %collective-permute-start.3) | collective-permute-done | bytes 1277984 | tf_op jit(solution)/shard_map/ppermute | solution.py:23
  79.5 2.1 select_bitcast_fusion.3
  81.6 1.7 pad_maximum_fusion.1
  83.4 2.1 slice.174
  88.5 2.2 select_bitcast_fusion.1
  91.9 1.4 multiply_reduce_fusion.1
  94.1 3.8 %constant_dynamic-update-slice_fusion.3 = (bf16[128,1792]{0,1:T(8,128)(2,1)S(1)}, f32[128,48]{0,1:T(8,128)S(1)}) fusion(bf16[128,1792]{0,1:T(8,128)(2,1)S(1)} %constant_dynamic-update-slice_fusion.4, f32[48]{0:T(128)S(1)} %convert_element_type.246, pred[128]{0:T(512)(128)(4,1)S(1)} %add_compare_fusion, s32[128]{0:T(128)S(1)} %get-tuple-element.63, ...), kind=kOutput, calls=%fused_computation.157 | convolution fusion | flops 2695168 | bytes 58880 | tf_op jit(solution)/shard_map/dot_general | solution.py:117
  98.0 2.0 constant_dynamic-update-slice_fusion.2
  100.0 1.6 collective-permute-start.5
  101.6 2.4 collective-permute-start.6
  104.0 3.4 %collective-permute-start.8 = (bf16[128,1792]{0,1:T(8,128)(2,1)S(1)}, bf16[128,1792]{0,1:T(8,128)(2,1)S(1)}, u32[]{:S(2)}, u32[]{:S(2)}) collective-permute-start(bf16[128,1792]{0,1:T(8,128)(2,1)S(1)} %constant_dynamic-update-slice_fusion), channel_id=1, source_target_pairs={{0,4},{1,5},{2,6},{3,7},{4,0},{5,1},{6,2},{7,3},{8,12},{9,13},{10,... | collective-permute-start | bytes 1376264 | tf_op jit(solution)/shard_map/ppermute | solution.py:155
  107.4 16.3 %collective-permute-done.8 = bf16[128,1792]{0,1:T(8,128)(2,1)S(1)} collective-permute-done((bf16[128,1792]{0,1:T(8,128)(2,1)S(1)}, bf16[128,1792]{0,1:T(8,128)(2,1)S(1)}, u32[]{:S(2)}, u32[]{:S(2)}) %collective-permute-start.8) | collective-permute-done | bytes 458784 | tf_op jit(solution)/shard_map/ppermute | solution.py:155
  124.2 4.4 %collective-permute-start.10 = (bf16[128,1792]{0,1:T(8,128)(2,1)S(1)}, bf16[128,1792]{0,1:T(8,128)(2,1)S(1)}, u32[]{:S(2)}, u32[]{:S(2)}) collective-permute-start(bf16[128,1792]{0,1:T(8,128)(2,1)S(1)} %collective-permute-done.8), channel_id=1, source_target_pairs={{0,2},{1,3},{2,0},{3,1},{4,6},{5,7},{6,4},{7,5},{8,10},{9,11},{10,... | collective-permute-start | bytes 1376264 | tf_op jit(solution)/shard_map/ppermute | solution.py:155
  128.6 1.5 collective-permute-start.7
  130.2 7.7 %collective-permute-done.10 = bf16[128,1792]{0,1:T(8,128)(2,1)S(1)} collective-permute-done((bf16[128,1792]{0,1:T(8,128)(2,1)S(1)}, bf16[128,1792]{0,1:T(8,128)(2,1)S(1)}, u32[]{:S(2)}, u32[]{:S(2)}) %collective-permute-start.10) | collective-permute-done | bytes 458784 | tf_op jit(solution)/shard_map/ppermute | solution.py:155
  138.0 1.5 collective-permute-start.11
  139.5 7.5 %collective-permute-done.7 = bf16[128,1792]{0,1:T(8,128)(2,1)S(1)} collective-permute-done((bf16[128,1792]{0,1:T(8,128)(2,1)S(1)}, bf16[128,1792]{0,1:T(8,128)(2,1)S(1)}, u32[]{:S(2)}, u32[]{:S(2)}) %collective-permute-start.7) | collective-permute-done | bytes 458784 | tf_op jit(solution)/shard_map/ppermute | solution.py:155
  147.3 7.5 %collective-permute-done.11 = bf16[128,1792]{0,1:T(8,128)(2,1)S(1)} collective-permute-done((bf16[128,1792]{0,1:T(8,128)(2,1)S(1)}, bf16[128,1792]{0,1:T(8,128)(2,1)S(1)}, u32[]{:S(2)}, u32[]{:S(2)}) %collective-permute-start.11) | collective-permute-done | bytes 458784 | tf_op jit(solution)/shard_map/ppermute | solution.py:155
  154.9 1.7 copy-done.9
  157.0 14.1 %fusion.16 = f32[8,6,32,1024]{3,2,0,1:T(8,128)} fusion(bf16[6,1536,1024]{2,1,0:T(8,128)(2,1)} %all-gather.4.cloned.1.call-done, bf16[8,128,1792]{1,2,0:T(8,128)(2,1)} %copy-done.9, f32[8,6,128]{2,1,0:T(8,128)S(1)} %get-tuple-element.48, f32[32]{0:T(128)S(1)} %iota_convert_fusion), kind=kOutput, calls=%fused_computation.21 | convolution fusion | flops 5438373888 | bytes 28336256 | tf_op jit(solution)/shard_map/hscd,sdf->hscf/dot_general | solution.py:173
  171.1 3.9 %fusion.10 = bf16[8,6,32,512]{3,2,0,1:T(8,128)(2,1)S(1)} fusion(f32[8,6,32,1024]{3,2,0,1:T(8,128)} %fusion.16), kind=kLoop, calls=%fused_computation.13 | loop fusion | flops 4718592 | bytes 7864320 | tf_op jit(solution)/shard_map/convert_element_type | solution.py:174
  175.0 5.6 %all-gather.6.cloned.1.call-done = bf16[6,1024,512]{2,1,0:T(8,128)(2,1)} async-done(((bf16[6,256,512]{2,1,0:T(8,128)(2,1)}), bf16[6,1024,512]{2,1,0:T(8,128)(2,1)}) %all-gather.6.cloned.1.call-update) | async-done | bytes 6291472 | tf_op jit(solution)/shard_map/all_gather | solution.py:85
  180.6 4.6 %fusion.3 = f32[6,8,32,1024]{3,2,0,1:T(8,128)S(1)} fusion(bf16[6,1024,512]{2,1,0:T(8,128)(2,1)} %all-gather.6.cloned.1.call-done, bf16[8,6,32,512]{3,2,0,1:T(8,128)(2,1)S(1)} %fusion.10), kind=kOutput, calls=%fused_computation.4 | convolution fusion | flops 1610612736 | bytes 14155776 | tf_op jit(solution)/shard_map/hscf,sdf->hscd/dot_general | solution.py:179
  186.3 1.5 collective-permute-start.13
  188.4 1.5 collective-permute-start.15
  189.8 5.6 %collective-permute-done.13 = bf16[128,1024]{1,0:T(8,128)(2,1)S(1)} collective-permute-done((bf16[128,1024]{1,0:T(8,128)(2,1)S(1)}, bf16[128,1024]{1,0:T(8,128)(2,1)S(1)}, u32[]{:S(2)}, u32[]{:S(2)}) %collective-permute-start.13) | collective-permute-done | bytes 262176 | tf_op jit(solution)/shard_map/ppermute | solution.py:34
  195.5 5.6 %collective-permute-done.16 = bf16[128,1024]{1,0:T(8,128)(2,1)S(1)} collective-permute-done((bf16[128,1024]{1,0:T(8,128)(2,1)S(1)}, bf16[128,1024]{1,0:T(8,128)(2,1)S(1)}, u32[]{:S(2)}, u32[]{:S(2)}) %collective-permute-start.16) | collective-permute-done | bytes 262176 | tf_op jit(solution)/shard_map/ppermute | solution.py:34
  201.3 1.5 collective-permute-start.17
  202.8 1.5 collective-permute-start.12
  204.9 1.8 collective-permute-done.15
  206.7 6.7 %collective-permute-done.17 = bf16[128,1024]{1,0:T(8,128)(2,1)S(1)} collective-permute-done((bf16[128,1024]{1,0:T(8,128)(2,1)S(1)}, bf16[128,1024]{1,0:T(8,128)(2,1)S(1)}, u32[]{:S(2)}, u32[]{:S(2)}) %collective-permute-start.17) | collective-permute-done | bytes 262176 | tf_op jit(solution)/shard_map/ppermute | solution.py:34
  213.6 3.3 %collective-permute-done.14 = bf16[128,1024]{1,0:T(8,128)(2,1)S(1)} collective-permute-done((bf16[128,1024]{1,0:T(8,128)(2,1)S(1)}, bf16[128,1024]{1,0:T(8,128)(2,1)S(1)}, u32[]{:S(2)}, u32[]{:S(2)}) %collective-permute-start.14) | collective-permute-done | bytes 262176 | tf_op jit(solution)/shard_map/ppermute | solution.py:34
  216.9 7.5 %collective-permute-done.18 = bf16[128,1024]{1,0:T(8,128)(2,1)S(1)} collective-permute-done((bf16[128,1024]{1,0:T(8,128)(2,1)S(1)}, bf16[128,1024]{1,0:T(8,128)(2,1)S(1)}, u32[]{:S(2)}, u32[]{:S(2)}) %collective-permute-start.18) | collective-permute-done | bytes 262176 | tf_op jit(solution)/shard_map/ppermute | solution.py:34
  224.5 4.3 %bitcast_convert_fusion.1 = bf16[8,128,512]{2,1,0:T(8,128)(2,1)} fusion(bf16[6,512,512]{2,1,0:T(8,128)(2,1)} %all-gather.8.cloned.1.call-done, f32[8,6,32]{2,1,0:T(8,128)S(1)} %select_reduce_fusion, bf16[8,6,32,512]{3,2,0,1:T(8,128)(2,1)S(1)} %fusion.10, f32[8,6,128]{2,1,0:T(8,128)S(1)} %get-tuple-element.48, f32[32]{0:T(128)S(1)} %iota_convert_fusion), kind=kOutput, calls=%fused_computation.29 | convolution fusion | flops 1008926720 | bytes 5798016 | tf_op jit(solution)/shard_map/hscr,hscd->hrd/dot_general | solution.py:181
  230.1 1.5 collective-permute-start.20
  232.2 1.5 collective-permute-start.22
  233.7 1.5 collective-permute-done.20
  235.2 2.8 %collective-permute-done.23 = bf16[128,512]{1,0:T(8,128)(2,1)S(1)} collective-permute-done((bf16[128,512]{1,0:T(8,128)(2,1)S(1)}, bf16[128,512]{1,0:T(8,128)(2,1)S(1)}, u32[]{:S(2)}, u32[]{:S(2)}) %collective-permute-start.23) | collective-permute-done | bytes 131104 | tf_op jit(solution)/shard_map/ppermute | solution.py:34
  239.8 1.3 collective-permute-start.19
  241.1 2.0 collective-permute-start.21
  245.1 1.6 broadcast_select_fusion
  246.9 4.9 %collective-permute-done.25 = bf16[128,512]{1,0:T(8,128)(2,1)S(1)} collective-permute-done((bf16[128,512]{1,0:T(8,128)(2,1)S(1)}, bf16[128,512]{1,0:T(8,128)(2,1)S(1)}, u32[]{:S(2)}, u32[]{:S(2)}) %collective-permute-start.25) | collective-permute-done | bytes 131104 | tf_op jit(solution)/shard_map/ppermute | solution.py:34
  (121 shorter events, 23.1 us)
Async XLA Ops:
  7.2 84.7 %copy-start = (bf16[128,1536]{1,0:T(8,128)(2,1)S(1)}, bf16[128,1536]{1,0:T(8,128)(2,1)}, u32[]{:S(2)}) copy-start(bf16[128,1536]{1,0:T(8,128)(2,1)} %param.18) | copy-start | bytes 1179652
  7.2 1.7 copy-start.4
  7.2 149.8 %all-gather.4.cloned.1.call-start = ((), (), s32[]{:S(2)}) async-start(), calls=%async_computation | async-start | bytes 23592960 | tf_op jit(solution)/shard_map/all_gather | solution.py:81
  7.9 2.3 copy-start.11
  7.9 2.4 copy-start.15
  7.9 2.5 copy-start.16
  8.0 2.6 copy-start.10
  8.0 172.6 %all-gather.6.cloned.1.call-start = ((), (), s32[]{:S(2)}) async-start(), calls=%async_computation.1 | async-start | bytes 7864320 | tf_op jit(solution)/shard_map/all_gather | solution.py:85
  10.2 214.4 %all-gather.8.cloned.1.call-start = ((), (), s32[]{:S(2)}) async-start(), calls=%async_computation.2 | async-start | bytes 3932160 | tf_op jit(solution)/shard_map/all_gather | solution.py:85
  10.7 7.1 %collective-permute-start = (bf16[48,1664]{1,0:T(8,128)(2,1)S(1)}, bf16[48,1664]{1,0:T(8,128)(2,1)S(1)}, u32[]{:S(2)}, u32[]{:S(2)}) collective-permute-start(bf16[48,1664]{1,0:T(8,128)(2,1)S(1)} %concatenate.9), channel_id=1, source_target_pairs={{0,16},{8,24},{16,0},{24,8},{1,17},{9,25},{17,1},{25,9},{2,18},{10... | collective-permute-start | bytes 479240 | tf_op jit(solution)/shard_map/ppermute | solution.py:23
  17.9 16.5 %collective-permute-start.1 = (bf16[2,48,1664]{2,1,0:T(8,128)(2,1)S(1)}, bf16[2,48,1664]{2,1,0:T(8,128)(2,1)S(1)}, u32[]{:S(2)}, u32[]{:S(2)}) collective-permute-start(bf16[2,48,1664]{2,1,0:T(8,128)(2,1)S(1)} %pad_maximum_fusion.5), channel_id=1, source_target_pairs={{0,4},{1,5},{2,6},{3,7},{4,0},{5,1},{6,2},{7,3},{8,12},{9,13},{10,... | collective-permute-start | bytes 958472 | tf_op jit(solution)/shard_map/ppermute | solution.py:23
  34.5 15.4 %collective-permute-start.2 = (bf16[2,2,48,1664]{3,2,1,0:T(8,128)(2,1)S(1)}, bf16[2,2,48,1664]{3,2,1,0:T(8,128)(2,1)S(1)}, u32[]{:S(2)}, u32[]{:S(2)}) collective-permute-start(bf16[2,2,48,1664]{3,2,1,0:T(8,128)(2,1)S(1)} %pad_maximum_fusion.4), channel_id=1, source_target_pairs={{0,2},{1,3},{2,0},{3,1},{4,6},{5,7},{6,4},{7,5},{8,10},{9,11},{10,... | collective-permute-start | bytes 1916936 | tf_op jit(solution)/shard_map/ppermute | solution.py:23
  50.0 0.9 copy-start.2
  50.1 1.0 copy-start.3
  51.1 28.4 %collective-permute-start.3 = (bf16[2,2,2,48,1664]{4,3,2,1,0:T(8,128)(2,1)S(1)}, bf16[2,2,2,48,1664]{4,3,2,1,0:T(8,128)(2,1)}, u32[]{:S(2)}, u32[]{:S(2)}) collective-permute-start(bf16[2,2,2,48,1664]{4,3,2,1,0:T(8,128)(2,1)S(1)} %pad_maximum_fusion.2), channel_id=1, source_target_pairs={{0,1},{1,0},{2,3},{3,2},{4,5},{5,4},{6,7},{7,6},{8,9},{9,8},{10,11... | collective-permute-start | bytes 3833864 | tf_op jit(solution)/shard_map/ppermute | solution.py:23
  81.6 3.9 %copy-start.6 = (bf16[128,1536]{1,0:T(8,128)(2,1)S(1)}, bf16[128,1536]{1,0:T(8,128)(2,1)}, u32[]{:S(2)}) copy-start(bf16[128,1536]{1,0:T(8,128)(2,1)} %param.19) | copy-start | bytes 1179652
  81.6 4.8 %copy-start.17 = (s32[48]{0:T(128)S(1)}, s32[48]{0:T(128)}, u32[]{:S(2)}) copy-start(s32[48]{0:T(128)} %param.31) | copy-start | bytes 580
  81.6 4.8 %copy-start.18 = (s32[5]{0:T(128)S(1)}, s32[5]{0:T(128)}, u32[]{:S(2)}) copy-start(s32[5]{0:T(128)} %param.29) | copy-start | bytes 64
  81.6 6.1 %copy-start.14 = (s32[48]{0:T(128)S(1)}, s32[48]{0:T(128)}, u32[]{:S(2)}) copy-start(s32[48]{0:T(128)} %param.30) | copy-start | bytes 580
  81.6 6.2 %copy-start.12 = (s32[128,8]{0,1:T(8,128)S(1)}, s32[128,8]{0,1:T(8,128)}, u32[]{:S(2)}) copy-start(s32[128,8]{0,1:T(8,128)} %param.28) | copy-start | bytes 12292
  81.6 6.2 %copy-start.13 = (s32[128,8]{0,1:T(8,128)S(1)}, s32[128,8]{0,1:T(8,128)}, u32[]{:S(2)}) copy-start(s32[128,8]{0,1:T(8,128)} %param.27) | copy-start | bytes 12292
  83.4 5.2 %collective-permute-start.4 = (bf16[2,2,2,2,48,1664]{5,4,3,2,1,0:T(8,128)(2,1)}, bf16[2,2,2,2,48,1664]{5,4,3,2,1,0:T(8,128)(2,1)}, u32[]{:S(2)}, u32[]{:S(2)}) collective-permute-start(bf16[2,2,2,2,48,1664]{5,4,3,2,1,0:T(8,128)(2,1)} %pad_maximum_fusion.1), channel_id=1, source_target_pairs={{0,8},{8,0},{16,24},{24,16},{1,9},{9,1},{17,25},{25,17},{2,10},{10... | collective-permute-start | bytes 7667720 | tf_op jit(solution)/shard_map/ppermute | solution.py:23
  90.8 1.1 copy-start.7
  100.0 30.1 %collective-permute-start.5 = (bf16[128,1792]{0,1:T(8,128)(2,1)S(1)}, bf16[128,1792]{0,1:T(8,128)(2,1)S(1)}, u32[]{:S(2)}, u32[]{:S(2)}) collective-permute-start(bf16[128,1792]{0,1:T(8,128)(2,1)S(1)} %constant_dynamic-update-slice_fusion), channel_id=1, source_target_pairs={{0,1},{1,0},{2,3},{3,2},{4,5},{5,4},{6,7},{7,6},{8,9},{9,8},{10,11... | collective-permute-start | bytes 1376264 | tf_op jit(solution)/shard_map/ppermute | solution.py:155
  101.6 27.0 %collective-permute-start.6 = (bf16[128,1792]{0,1:T(8,128)(2,1)S(1)}, bf16[128,1792]{0,1:T(8,128)(2,1)S(1)}, u32[]{:S(2)}, u32[]{:S(2)}) collective-permute-start(bf16[128,1792]{0,1:T(8,128)(2,1)S(1)} %constant_dynamic-update-slice_fusion), channel_id=1, source_target_pairs={{0,2},{1,3},{2,0},{3,1},{4,6},{5,7},{6,4},{7,5},{8,10},{9,11},{10,... | collective-permute-start | bytes 1376264 | tf_op jit(solution)/shard_map/ppermute | solution.py:155
  104.0 19.7 %collective-permute-start.8 = (bf16[128,1792]{0,1:T(8,128)(2,1)S(1)}, bf16[128,1792]{0,1:T(8,128)(2,1)S(1)}, u32[]{:S(2)}, u32[]{:S(2)}) collective-permute-start(bf16[128,1792]{0,1:T(8,128)(2,1)S(1)} %constant_dynamic-update-slice_fusion), channel_id=1, source_target_pairs={{0,4},{1,5},{2,6},{3,7},{4,0},{5,1},{6,2},{7,3},{8,12},{9,13},{10,... | collective-permute-start | bytes 1376264 | tf_op jit(solution)/shard_map/ppermute | solution.py:155
  123.7 23.4 %collective-permute-start.9 = (bf16[128,1792]{0,1:T(8,128)(2,1)S(1)}, bf16[128,1792]{0,1:T(8,128)(2,1)S(1)}, u32[]{:S(2)}, u32[]{:S(2)}) collective-permute-start(bf16[128,1792]{0,1:T(8,128)(2,1)S(1)} %collective-permute-done.8), channel_id=1, source_target_pairs={{0,1},{1,0},{2,3},{3,2},{4,5},{5,4},{6,7},{7,6},{8,9},{9,8},{10,11... | collective-permute-start | bytes 1376264 | tf_op jit(solution)/shard_map/ppermute | solution.py:155
  124.2 13.8 %collective-permute-start.10 = (bf16[128,1792]{0,1:T(8,128)(2,1)S(1)}, bf16[128,1792]{0,1:T(8,128)(2,1)S(1)}, u32[]{:S(2)}, u32[]{:S(2)}) collective-permute-start(bf16[128,1792]{0,1:T(8,128)(2,1)S(1)} %collective-permute-done.8), channel_id=1, source_target_pairs={{0,2},{1,3},{2,0},{3,1},{4,6},{5,7},{6,4},{7,5},{8,10},{9,11},{10,... | collective-permute-start | bytes 1376264 | tf_op jit(solution)/shard_map/ppermute | solution.py:155
  128.6 18.4 %collective-permute-start.7 = (bf16[128,1792]{0,1:T(8,128)(2,1)S(1)}, bf16[128,1792]{0,1:T(8,128)(2,1)S(1)}, u32[]{:S(2)}, u32[]{:S(2)}) collective-permute-start(bf16[128,1792]{0,1:T(8,128)(2,1)S(1)} %collective-permute-done.6), channel_id=1, source_target_pairs={{0,1},{1,0},{2,3},{3,2},{4,5},{5,4},{6,7},{7,6},{8,9},{9,8},{10,11... | collective-permute-start | bytes 1376264 | tf_op jit(solution)/shard_map/ppermute | solution.py:155
  138.0 16.8 %collective-permute-start.11 = (bf16[128,1792]{0,1:T(8,128)(2,1)S(1)}, bf16[128,1792]{0,1:T(8,128)(2,1)S(1)}, u32[]{:S(2)}, u32[]{:S(2)}) collective-permute-start(bf16[128,1792]{0,1:T(8,128)(2,1)S(1)} %collective-permute-done.10), channel_id=1, source_target_pairs={{0,1},{1,0},{2,3},{3,2},{4,5},{5,4},{6,7},{7,6},{8,9},{9,8},{10,11... | collective-permute-start | bytes 1376264 | tf_op jit(solution)/shard_map/ppermute | solution.py:155
  154.8 1.8 copy-start.9
  186.3 9.2 %collective-permute-start.13 = (bf16[128,1024]{1,0:T(8,128)(2,1)S(1)}, bf16[128,1024]{1,0:T(8,128)(2,1)S(1)}, u32[]{:S(2)}, u32[]{:S(2)}) collective-permute-start(bf16[128,1024]{1,0:T(8,128)(2,1)S(1)} %get-tuple-element.30), channel_id=1, source_target_pairs={{0,1},{1,0},{2,3},{3,2},{4,5},{5,4},{6,7},{7,6},{8,9},{9,8},{10,11... | collective-permute-start | bytes 786440 | tf_op jit(solution)/shard_map/ppermute | solution.py:34
  187.8 13.3 %collective-permute-start.16 = (bf16[128,1024]{1,0:T(8,128)(2,1)S(1)}, bf16[128,1024]{1,0:T(8,128)(2,1)S(1)}, u32[]{:S(2)}, u32[]{:S(2)}) collective-permute-start(bf16[128,1024]{1,0:T(8,128)(2,1)S(1)} %get-tuple-element.28), channel_id=1, source_target_pairs={{0,1},{1,0},{2,3},{3,2},{4,5},{5,4},{6,7},{7,6},{8,9},{9,8},{10,11... | collective-permute-start | bytes 786440 | tf_op jit(solution)/shard_map/ppermute | solution.py:34
  188.4 18.3 %collective-permute-start.15 = (bf16[128,1024]{1,0:T(8,128)(2,1)S(1)}, bf16[128,1024]{1,0:T(8,128)(2,1)S(1)}, u32[]{:S(2)}, u32[]{:S(2)}) collective-permute-start(bf16[128,1024]{1,0:T(8,128)(2,1)S(1)} %get-tuple-element.29), channel_id=1, source_target_pairs={{0,1},{1,0},{2,3},{3,2},{4,5},{5,4},{6,7},{7,6},{8,9},{9,8},{10,11... | collective-permute-start | bytes 786440 | tf_op jit(solution)/shard_map/ppermute | solution.py:34
  201.3 12.1 %collective-permute-start.17 = (bf16[128,1024]{1,0:T(8,128)(2,1)S(1)}, bf16[128,1024]{1,0:T(8,128)(2,1)S(1)}, u32[]{:S(2)}, u32[]{:S(2)}) collective-permute-start(bf16[128,1024]{1,0:T(8,128)(2,1)S(1)} %get-tuple-element.32), channel_id=1, source_target_pairs={{0,2},{1,3},{2,0},{3,1},{4,6},{5,7},{6,4},{7,5},{8,10},{9,11},{10,... | collective-permute-start | bytes 786440 | tf_op jit(solution)/shard_map/ppermute | solution.py:34
  202.8 10.8 %collective-permute-start.12 = (bf16[128,1024]{1,0:T(8,128)(2,1)S(1)}, bf16[128,1024]{1,0:T(8,128)(2,1)S(1)}, u32[]{:S(2)}, u32[]{:S(2)}) collective-permute-start(bf16[128,1024]{1,0:T(8,128)(2,1)S(1)} %get-tuple-element.27), channel_id=1, source_target_pairs={{0,1},{1,0},{2,3},{3,2},{4,5},{5,4},{6,7},{7,6},{8,9},{9,8},{10,11... | collective-permute-start | bytes 786440 | tf_op jit(solution)/shard_map/ppermute | solution.py:34
  204.3 12.6 %collective-permute-start.14 = (bf16[128,1024]{1,0:T(8,128)(2,1)S(1)}, bf16[128,1024]{1,0:T(8,128)(2,1)S(1)}, u32[]{:S(2)}, u32[]{:S(2)}) collective-permute-start(bf16[128,1024]{1,0:T(8,128)(2,1)S(1)} %get-tuple-element.31), channel_id=1, source_target_pairs={{0,2},{1,3},{2,0},{3,1},{4,6},{5,7},{6,4},{7,5},{8,10},{9,11},{10,... | collective-permute-start | bytes 786440 | tf_op jit(solution)/shard_map/ppermute | solution.py:34
  213.5 10.8 %collective-permute-start.18 = (bf16[128,1024]{1,0:T(8,128)(2,1)S(1)}, bf16[128,1024]{1,0:T(8,128)(2,1)S(1)}, u32[]{:S(2)}, u32[]{:S(2)}) collective-permute-start(bf16[128,1024]{1,0:T(8,128)(2,1)S(1)} %add_convert_fusion), channel_id=1, source_target_pairs={{0,4},{1,5},{2,6},{3,7},{4,0},{5,1},{6,2},{7,3},{8,12},{9,13},{10,... | collective-permute-start | bytes 786440 | tf_op jit(solution)/shard_map/ppermute | solution.py:34
  224.5 20.6 %copy-start.8 = (bf16[128,1024]{1,0:T(8,128)(2,1)S(1)}, bf16[128,1024]{1,0:T(8,128)(2,1)}, u32[]{:S(2)}) copy-start(bf16[128,1024]{1,0:T(8,128)(2,1)} %param.20) | copy-start | bytes 786436
  228.9 16.3 %copy-start.5 = (bf16[8,128,1024]{2,1,0:T(8,128)(2,1)S(1)}, bf16[8,128,1024]{2,1,0:T(8,128)(2,1)}, u32[]{:S(2)}) copy-start(bf16[8,128,1024]{2,1,0:T(8,128)(2,1)} %param.21) | copy-start | bytes 6291460
  230.1 5.0 %collective-permute-start.20 = (bf16[128,512]{1,0:T(8,128)(2,1)S(1)}, bf16[128,512]{1,0:T(8,128)(2,1)S(1)}, u32[]{:S(2)}, u32[]{:S(2)}) collective-permute-start(bf16[128,512]{1,0:T(8,128)(2,1)S(1)} %get-tuple-element.40), channel_id=1, source_target_pairs={{0,1},{1,0},{2,3},{3,2},{4,5},{5,4},{6,7},{7,6},{8,9},{9,8},{10,11... | collective-permute-start | bytes 393224 | tf_op jit(solution)/shard_map/ppermute | solution.py:34
  231.7 6.3 %collective-permute-start.23 = (bf16[128,512]{1,0:T(8,128)(2,1)S(1)}, bf16[128,512]{1,0:T(8,128)(2,1)S(1)}, u32[]{:S(2)}, u32[]{:S(2)}) collective-permute-start(bf16[128,512]{1,0:T(8,128)(2,1)S(1)} %get-tuple-element.38), channel_id=1, source_target_pairs={{0,1},{1,0},{2,3},{3,2},{4,5},{5,4},{6,7},{7,6},{8,9},{9,8},{10,11... | collective-permute-start | bytes 393224 | tf_op jit(solution)/shard_map/ppermute | solution.py:34
  232.2 10.9 %collective-permute-start.22 = (bf16[128,512]{1,0:T(8,128)(2,1)S(1)}, bf16[128,512]{1,0:T(8,128)(2,1)S(1)}, u32[]{:S(2)}, u32[]{:S(2)}) collective-permute-start(bf16[128,512]{1,0:T(8,128)(2,1)S(1)} %get-tuple-element.39), channel_id=1, source_target_pairs={{0,1},{1,0},{2,3},{3,2},{4,5},{5,4},{6,7},{7,6},{8,9},{9,8},{10,11... | collective-permute-start | bytes 393224 | tf_op jit(solution)/shard_map/ppermute | solution.py:34
  239.0 5.0 %collective-permute-start.24 = (bf16[128,512]{1,0:T(8,128)(2,1)S(1)}, bf16[128,512]{1,0:T(8,128)(2,1)S(1)}, u32[]{:S(2)}, u32[]{:S(2)}) collective-permute-start(bf16[128,512]{1,0:T(8,128)(2,1)S(1)} %get-tuple-element.42), channel_id=1, source_target_pairs={{0,2},{1,3},{2,0},{3,1},{4,6},{5,7},{6,4},{7,5},{8,10},{9,11},{10,... | collective-permute-start | bytes 393224 | tf_op jit(solution)/shard_map/ppermute | solution.py:34
  239.8 7.2 %collective-permute-start.19 = (bf16[128,512]{1,0:T(8,128)(2,1)S(1)}, bf16[128,512]{1,0:T(8,128)(2,1)S(1)}, u32[]{:S(2)}, u32[]{:S(2)}) collective-permute-start(bf16[128,512]{1,0:T(8,128)(2,1)S(1)} %get-tuple-element.37), channel_id=1, source_target_pairs={{0,1},{1,0},{2,3},{3,2},{4,5},{5,4},{6,7},{7,6},{8,9},{9,8},{10,11... | collective-permute-start | bytes 393224 | tf_op jit(solution)/shard_map/ppermute | solution.py:34
  241.1 5.8 %collective-permute-start.21 = (bf16[128,512]{1,0:T(8,128)(2,1)S(1)}, bf16[128,512]{1,0:T(8,128)(2,1)S(1)}, u32[]{:S(2)}, u32[]{:S(2)}) collective-permute-start(bf16[128,512]{1,0:T(8,128)(2,1)S(1)} %get-tuple-element.41), channel_id=1, source_target_pairs={{0,2},{1,3},{2,0},{3,1},{4,6},{5,7},{6,4},{7,5},{8,10},{9,11},{10,... | collective-permute-start | bytes 393224 | tf_op jit(solution)/shard_map/ppermute | solution.py:34
  245.0 6.8 %collective-permute-start.25 = (bf16[128,512]{1,0:T(8,128)(2,1)S(1)}, bf16[128,512]{1,0:T(8,128)(2,1)S(1)}, u32[]{:S(2)}, u32[]{:S(2)}) collective-permute-start(bf16[128,512]{1,0:T(8,128)(2,1)S(1)} %add_convert_fusion.2), channel_id=1, source_target_pairs={{0,4},{1,5},{2,6},{3,7},{4,0},{5,1},{6,2},{7,3},{8,12},{9,13},{10,... | collective-permute-start | bytes 393224 | tf_op jit(solution)/shard_map/ppermute | solution.py:34
  252.9 2.4 copy-start.1
Sparse Core Ops, SparseCore 0:
  9.6 122.3 all-gather.3
  134.2 46.3 all-gather.5
  182.2 28.5 all-gather.7

commit v3 on v2

--- a/solution.py
+++ b/solution.py
@@ -11,11 +11,14 @@
     return values * lax.rsqrt(mean_sq + eps_norm) * gain.astype(jnp.float32)
 
 
-def spread_by_doubling(block, bits):
+def spread_by_doubling(block, bits, low_first):
     dp_bits = [1 << level for level in range(lax.axis_size("dp").bit_length() - 1)]
     outer = len(dp_bits) - 1 if dp_bits else 0
     steps = [("dp", bit, at) for at, bit in enumerate(reversed(dp_bits[1:]))]
-    steps += [("expert", bit, outer + at) for at, bit in enumerate(reversed(bits))]
+    expert_steps = [("expert", bit, outer + at) for at, bit in enumerate(reversed(bits))]
+    if low_first and bits:
+        expert_steps = [("expert", bits[0], outer)] + expert_steps[:-1]
+    steps += expert_steps
     steps += [("dp", bit, outer) for bit in dp_bits[:1]]
     held = block
     for name, bit, at in steps:
@@ -69,7 +72,7 @@
     side = -(-(experts_all + 2) // 128) * 128
     packed = jnp.concatenate(
         [
-            out_weight,
+            out_weight[:, row_width // 2 :],
             router,
             attn_gain[:, None],
             ffn_gain[:, None],
@@ -77,11 +80,12 @@
         ],
         axis=1,
     )
-    packed_full = spread_by_doubling(packed, bits)
+    half = row_width // 2
+    left_full = spread_by_doubling(out_weight[:, :half], bits, False)
+    right_full = spread_by_doubling(packed, bits, True)
     w_in = lax.all_gather(slot_in, "dp", axis=1, tiled=True)
     features = slot_out.shape[1]
-    first = min(features, -(-features // 256) * 128)
-    cuts = [(0, first), (first, features)] if first < features else [(0, features)]
+    cuts = [(lo, min(lo + 128, features)) for lo in range(0, features, 128)]
     w_out = [lax.all_gather(slot_out[:, lo:hi], "dp", axis=1, tiled=True) for lo, hi in cuts]
 
     page_rows = kv_pool.shape[1]
@@ -120,12 +124,17 @@
     kept = chosen & (position < slot_capacity[None, :].astype(jnp.float32))
     place = jnp.where(kept, position, -1.0).astype(jnp.bfloat16)
 
-    proj = jnp.dot(
-        attended, packed_full[:, :row_width], preferred_element_type=jnp.float32
-    )
-    gain_first = packed_full[:, row_width + experts_all]
-    gain_second = packed_full[:, row_width + experts_all + 1]
-    router_full = packed_full[:, row_width : row_width + experts_all]
+    rest = row_width - half
+    proj = jnp.concatenate(
+        [
+            jnp.dot(attended, left_full, preferred_element_type=jnp.float32),
+            jnp.dot(attended, right_full[:, :rest], preferred_element_type=jnp.float32),
+        ],
+        axis=1,
+    )
+    gain_first = right_full[:, rest + experts_all]
+    gain_second = right_full[:, rest + experts_all + 1]
+    router_full = right_full[:, rest : rest + experts_all]
     hidden = (residual.astype(jnp.float32) + proj).astype(jnp.bfloat16)
     normed = rms_scale(hidden.astype(jnp.float32), gain_first).astype(jnp.bfloat16)
     logits = jnp.dot(normed, router_full, preferred_element_type=jnp.float32)

time: 262 us -> 262 us (level)
  waiting for transfers between devices: 146 us -> 129 us
  starting transfers between devices: 37.7 us -> 53.8 us
    ppermute x5 -> x10, waiting for transfers between devices: 60.1 us -> 30.7 us  [spread_by_doubling(): came = lax.ppermute(held, name, pairs)]
    ppermute x14 -> x21, starting transfers between devices: 14.3 us -> 28.9 us  [halve_sums(): came = lax.ppermute(sums[key], 'expert', pairs)]
    all_gather x2 -> x3, waiting for transfers between devices: 5.61 us -> 18.2 us  [on_device(): lax.all_gather(slot_out[:, lo:hi], 'dp', axis=1, tiled=True)]
    ppermute x5 -> x10, starting transfers between devices: 7.98 us -> 15.5 us  [spread_by_doubling(): came = lax.ppermute(held, name, pairs)]
    ppermute x7, starting transfers between devices: 15.3 us -> 9.23 us  [on_device(): blocks[key ^ bit] = lax.ppermute(blocks[key], 'expert', pairs)]
    ppermute x14 -> x21, waiting for transfers between devices: 40.6 us -> 34.9 us  [halve_sums(): came = lax.ppermute(sums[key], 'expert', pairs)]
    dot_general x2 -> x3, matrix products: 5.29 us -> 10.8 us  [on_device(): jnp.einsum('hscr,hscd->hrd', hot_low, scaled, preferred_element_type=jnp....]
    ppermute x7, waiting for transfers between devices: 39 us -> 43.9 us  [on_device(): blocks[key ^ bit] = lax.ppermute(blocks[key], 'expert', pairs)]
  transfers between devices with their start and end apart: 29 -> 42, of which waited for: 20 -> 27; matrix products, arithmetic and copies ran while one was open for 19% -> 20% of each run, Pallas kernels for 0% -> 0%
where the time goes in v3:
time: 262 us; the launch traced here: 261 us
  waiting for transfers between devices  129 us (49%)
  starting transfers between devices  53.8 us (21%)
  matrix products  33 us (13%)
  other arithmetic  19.8 us (8%)
  between operations  15.1 us (6%)
  local copies, waits for them, and re-layouts  9.88 us (4%)
    ppermute x7, waiting for transfers between devices, on_device(): blocks[key ^ bit] = lax.ppermute(blocks[key], 'expert', pairs)  43.9 us
    ppermute x21, waiting for transfers between devices, halve_sums(): came = lax.ppermute(sums[key], 'expert', pairs)  34.9 us
    ppermute x10, waiting for transfers between devices, spread_by_doubling(): came = lax.ppermute(held, name, pairs)  30.7 us
    ppermute x21, starting transfers between devices, halve_sums(): came = lax.ppermute(sums[key], 'expert', pairs)  28.9 us
    all_gather x3, waiting for transfers between devices, on_device(): lax.all_gather(slot_out[:, lo:hi], 'dp', axis=1, tiled=True)  18.2 us
    ppermute x10, starting transfers between devices, spread_by_doubling(): came = lax.ppermute(held, name, pairs)  15.5 us
    dot_general x1, matrix products, on_device(): jnp.einsum('hscd,sdf->hscf', rows_in, w_in, preferred_element_type=jnp.fl...  14.1 us
    dot_general x3, matrix products, on_device(): jnp.einsum('hscr,hscd->hrd', hot_low, scaled, preferred_element_type=jnp....  10.8 us
  transfers between devices with their start and end apart: 42, of which 27 were waited for; matrix products, arithmetic and copies ran while one was open for 20% of the time, Pallas kernels for 0%

profile of v3, /device:TPU:0, one launch (start us, length us, event | category | flops | bytes accessed | tf_op | source)
XLA Modules:
  0.0 260.6 jit_solution(4367915577353175213)
XLA Ops:
  11.2 3.0 %collective-permute-start = (bf16[48,768]{1,0:T(8,128)(2,1)S(1)}, bf16[48,768]{1,0:T(8,128)(2,1)S(1)}, u32[]{:S(2)}, u32[]{:S(2)}) collective-permute-start(bf16[48,768]{1,0:T(8,128)(2,1)S(1)} %slice.171), channel_id=1, source_target_pairs={{0,16},{8,24},{16,0},{24,8},{1,17},{9,25},{17,1},{25,9},{2,18},{10... | collective-permute-start | bytes 221192 | tf_op jit(solution)/shard_map/ppermute | solution.py:26
  14.7 1.9 collective-permute-done
  16.7 2.1 collective-permute-start.5
  18.8 2.7 %collective-permute-start.1 = (bf16[2,48,768]{2,1,0:T(8,128)(2,1)S(1)}, bf16[2,48,768]{2,1,0:T(8,128)(2,1)S(1)}, u32[]{:S(2)}, u32[]{:S(2)}) collective-permute-start(bf16[2,48,768]{2,1,0:T(8,128)(2,1)S(1)} %pad_maximum_fusion.10), channel_id=1, source_target_pairs={{0,4},{1,5},{2,6},{3,7},{4,0},{5,1},{6,2},{7,3},{8,12},{9,13},{10,... | collective-permute-start | bytes 442376 | tf_op jit(solution)/shard_map/ppermute | solution.py:26
  21.5 1.9 collective-permute-start.6
  23.4 3.7 %collective-permute-done.1 = bf16[2,48,768]{2,1,0:T(8,128)(2,1)S(1)} collective-permute-done((bf16[2,48,768]{2,1,0:T(8,128)(2,1)S(1)}, bf16[2,48,768]{2,1,0:T(8,128)(2,1)S(1)}, u32[]{:S(2)}, u32[]{:S(2)}) %collective-permute-start.1) | collective-permute-done | bytes 147488 | tf_op jit(solution)/shard_map/ppermute | solution.py:26
  27.9 3.4 %collective-permute-start.7 = (bf16[2,2,48,896]{3,2,1,0:T(8,128)(2,1)S(1)}, bf16[2,2,48,896]{3,2,1,0:T(8,128)(2,1)S(1)}, u32[]{:S(2)}, u32[]{:S(2)}) collective-permute-start(bf16[2,2,48,896]{3,2,1,0:T(8,128)(2,1)S(1)} %pad_maximum_fusion.7), channel_id=1, source_target_pairs={{0,4},{1,5},{2,6},{3,7},{4,0},{5,1},{6,2},{7,3},{8,12},{9,13},{10,... | collective-permute-start | bytes 1032200 | tf_op jit(solution)/shard_map/ppermute | solution.py:26
  31.4 8.5 %collective-permute-done.2 = bf16[2,2,48,768]{3,2,1,0:T(8,128)(2,1)S(1)} collective-permute-done((bf16[2,2,48,768]{3,2,1,0:T(8,128)(2,1)S(1)}, bf16[2,2,48,768]{3,2,1,0:T(8,128)(2,1)S(1)}, u32[]{:S(2)}, u32[]{:S(2)}) %collective-permute-start.2) | collective-permute-done | bytes 294944 | tf_op jit(solution)/shard_map/ppermute | solution.py:26
  40.0 1.6 collective-permute-start.3
  41.6 4.2 %collective-permute-done.7 = bf16[2,2,48,896]{3,2,1,0:T(8,128)(2,1)S(1)} collective-permute-done((bf16[2,2,48,896]{3,2,1,0:T(8,128)(2,1)S(1)}, bf16[2,2,48,896]{3,2,1,0:T(8,128)(2,1)S(1)}, u32[]{:S(2)}, u32[]{:S(2)}) %collective-permute-start.7) | collective-permute-done | bytes 344096 | tf_op jit(solution)/shard_map/ppermute | solution.py:26
  46.1 3.9 %collective-permute-done.3 = bf16[2,2,2,48,768]{4,3,2,1,0:T(8,128)(2,1)S(1)} collective-permute-done((bf16[2,2,2,48,768]{4,3,2,1,0:T(8,128)(2,1)S(1)}, bf16[2,2,2,48,768]{4,3,2,1,0:T(8,128)(2,1)S(1)}, u32[]{:S(2)}, u32[]{:S(2)}) %collective-permute-start.3) | collective-permute-done | bytes 589856 | tf_op jit(solution)/shard_map/ppermute | solution.py:26
  51.9 8.6 %collective-permute-done.8 = bf16[2,2,2,48,896]{4,3,2,1,0:T(8,128)(2,1)S(1)} collective-permute-done((bf16[2,2,2,48,896]{4,3,2,1,0:T(8,128)(2,1)S(1)}, bf16[2,2,2,48,896]{4,3,2,1,0:T(8,128)(2,1)S(1)}, u32[]{:S(2)}, u32[]{:S(2)}) %collective-permute-start.8) | collective-permute-done | bytes 688160 | tf_op jit(solution)/shard_map/ppermute | solution.py:26
  66.3 1.6 select_bitcast_fusion.1
  70.6 3.8 %constant_dynamic-update-slice_fusion.3 = (bf16[128,1792]{0,1:T(8,128)(2,1)S(1)}, f32[128,48]{0,1:T(8,128)S(1)}) fusion(bf16[128,1792]{0,1:T(8,128)(2,1)S(1)} %fusion.75, f32[48]{0:T(128)S(1)} %convert_element_type.324, pred[128]{0:T(512)(128)(4,1)S(1)} %add_compare_fusion, s32[128]{0:T(128)S(1)} %get-tuple-element.91, s32[128]{0:T(128)S(1)} %get-tuple-element.100, ...), kind=kOutput, calls=%fused_computation.205 | convolution fusion | flops 2695168 | bytes 58880 | tf_op jit(solution)/shard_map/dot_general | solution.py:121
  74.5 2.2 constant_dynamic-update-slice_fusion.2
  76.6 1.6 collective-permute-start.10
  78.6 3.4 %collective-permute-start.13 = (bf16[128,1792]{0,1:T(8,128)(2,1)S(1)}, bf16[128,1792]{0,1:T(8,128)(2,1)S(1)}, u32[]{:S(2)}, u32[]{:S(2)}) collective-permute-start(bf16[128,1792]{0,1:T(8,128)(2,1)S(1)} %constant_dynamic-update-slice_fusion), channel_id=1, source_target_pairs={{0,4},{1,5},{2,6},{3,7},{4,0},{5,1},{6,2},{7,3},{8,12},{9,13},{10,... | collective-permute-start | bytes 1376264 | tf_op jit(solution)/shard_map/ppermute | solution.py:164
  82.0 20.6 %collective-permute-done.13 = bf16[128,1792]{0,1:T(8,128)(2,1)S(1)} collective-permute-done((bf16[128,1792]{0,1:T(8,128)(2,1)S(1)}, bf16[128,1792]{0,1:T(8,128)(2,1)S(1)}, u32[]{:S(2)}, u32[]{:S(2)}) %collective-permute-start.13) | collective-permute-done | bytes 458784 | tf_op jit(solution)/shard_map/ppermute | solution.py:164
  105.1 8.2 %collective-permute-done.15 = bf16[128,1792]{0,1:T(8,128)(2,1)S(1)} collective-permute-done((bf16[128,1792]{0,1:T(8,128)(2,1)S(1)}, bf16[128,1792]{0,1:T(8,128)(2,1)S(1)}, u32[]{:S(2)}, u32[]{:S(2)}) %collective-permute-start.15) | collective-permute-done | bytes 458784 | tf_op jit(solution)/shard_map/ppermute | solution.py:164
  113.2 1.6 collective-permute-start.16
  114.8 10.6 %collective-permute-done.12 = bf16[128,1792]{0,1:T(8,128)(2,1)S(1)} collective-permute-done((bf16[128,1792]{0,1:T(8,128)(2,1)S(1)}, bf16[128,1792]{0,1:T(8,128)(2,1)S(1)}, u32[]{:S(2)}, u32[]{:S(2)}) %collective-permute-start.12) | collective-permute-done | bytes 458784 | tf_op jit(solution)/shard_map/ppermute | solution.py:164
  125.6 4.6 %collective-permute-done.16 = bf16[128,1792]{0,1:T(8,128)(2,1)S(1)} collective-permute-done((bf16[128,1792]{0,1:T(8,128)(2,1)S(1)}, bf16[128,1792]{0,1:T(8,128)(2,1)S(1)}, u32[]{:S(2)}, u32[]{:S(2)}) %collective-permute-start.16) | collective-permute-done | bytes 458784 | tf_op jit(solution)/shard_map/ppermute | solution.py:164
  130.4 1.8 copy-done.7
  132.5 14.1 %fusion.14 = f32[8,6,32,1024]{3,2,0,1:T(8,128)} fusion(bf16[6,1536,1024]{2,1,0:T(8,128)(2,1)} %all-gather.5.cloned.1.call-done, bf16[8,128,1792]{1,2,0:T(8,128)(2,1)} %copy-done.7, f32[8,6,128]{2,1,0:T(8,128)S(1)} %get-tuple-element.75, f32[32]{0:T(128)S(1)} %iota_convert_fusion), kind=kOutput, calls=%fused_computation.20 | convolution fusion | flops 5438373888 | bytes 28336256 | tf_op jit(solution)/shard_map/hscd,sdf->hscf/dot_general | solution.py:182
  146.6 3.9 %fusion.3 = bf16[8,6,32,512]{3,2,0,1:T(8,128)(2,1)S(1)} fusion(f32[8,6,32,1024]{3,2,0,1:T(8,128)} %fusion.14), kind=kLoop, calls=%fused_computation.4 | loop fusion | flops 4718592 | bytes 7864320 | tf_op jit(solution)/shard_map/convert_element_type | solution.py:183
  150.5 11.7 %all-gather.7.cloned.1.call-done = bf16[6,512,512]{2,1,0:T(8,128)(2,1)} async-done(((bf16[6,128,512]{2,1,0:T(8,128)(2,1)}), bf16[6,512,512]{2,1,0:T(8,128)(2,1)}) %all-gather.7.cloned.1.call-update) | async-done | bytes 3145744 | tf_op jit(solution)/shard_map/all_gather | solution.py:89
  162.2 3.3 %bitcast_convert_fusion.2 = bf16[8,128,512]{2,1,0:T(8,128)(2,1)S(1)} fusion(bf16[6,512,512]{2,1,0:T(8,128)(2,1)} %all-gather.7.cloned.1.call-done, f32[8,6,32]{2,1,0:T(8,128)S(1)} %fusion.48, bf16[8,6,32,512]{3,2,0,1:T(8,128)(2,1)S(1)} %fusion.3, f32[8,6,128]{2,1,0:T(8,128)S(1)} %get-tuple-element.75, f32[32]{0:T(128)S(1)} %iota_convert_fusion), kind=kOutput, calls=%fused_computation.26 | convolution fusion | flops 1008926720 | bytes 5798016 | tf_op jit(solution)/shard_map/hscr,hscd->hrd/dot_general | solution.py:190
  169.0 2.8 %collective-permute-done.18 = bf16[128,512]{1,0:T(8,128)(2,1)S(1)} collective-permute-done((bf16[128,512]{1,0:T(8,128)(2,1)S(1)}, bf16[128,512]{1,0:T(8,128)(2,1)S(1)}, u32[]{:S(2)}, u32[]{:S(2)}) %collective-permute-start.18) | collective-permute-done | bytes 131104 | tf_op jit(solution)/shard_map/ppermute | solution.py:37
  171.9 2.8 %collective-permute-done.21 = bf16[128,512]{1,0:T(8,128)(2,1)S(1)} collective-permute-done((bf16[128,512]{1,0:T(8,128)(2,1)S(1)}, bf16[128,512]{1,0:T(8,128)(2,1)S(1)}, u32[]{:S(2)}, u32[]{:S(2)}) %collective-permute-start.21) | collective-permute-done | bytes 131104 | tf_op jit(solution)/shard_map/ppermute | solution.py:37
  178.3 2.7 %collective-permute-done.22 = bf16[128,512]{1,0:T(8,128)(2,1)S(1)} collective-permute-done((bf16[128,512]{1,0:T(8,128)(2,1)S(1)}, bf16[128,512]{1,0:T(8,128)(2,1)S(1)}, u32[]{:S(2)}, u32[]{:S(2)}) %collective-permute-start.22) | collective-permute-done | bytes 131104 | tf_op jit(solution)/shard_map/ppermute | solution.py:37
  181.1 2.5 collective-permute-start.23
  184.2 4.3 %collective-permute-done.23 = bf16[128,512]{1,0:T(8,128)(2,1)S(1)} collective-permute-done((bf16[128,512]{1,0:T(8,128)(2,1)S(1)}, bf16[128,512]{1,0:T(8,128)(2,1)S(1)}, u32[]{:S(2)}, u32[]{:S(2)}) %collective-permute-start.23) | collective-permute-done | bytes 131104 | tf_op jit(solution)/shard_map/ppermute | solution.py:37
  188.5 3.8 %all-gather.9.cloned.1.call-done = bf16[6,512,512]{2,1,0:T(8,128)(2,1)} async-done(((bf16[6,128,512]{2,1,0:T(8,128)(2,1)}), bf16[6,512,512]{2,1,0:T(8,128)(2,1)}) %all-gather.9.cloned.1.call-update) | async-done | bytes 3145744 | tf_op jit(solution)/shard_map/all_gather | solution.py:89
  192.3 3.3 %bitcast_convert_fusion.1 = bf16[8,128,512]{2,1,0:T(8,128)(2,1)S(1)} fusion(bf16[6,512,512]{2,1,0:T(8,128)(2,1)} %all-gather.9.cloned.1.call-done, f32[8,6,32]{2,1,0:T(8,128)S(1)} %fusion.48, bf16[8,6,32,512]{3,2,0,1:T(8,128)(2,1)S(1)} %fusion.3, f32[8,6,128]{2,1,0:T(8,128)S(1)} %get-tuple-element.75, f32[32]{0:T(128)S(1)} %iota_convert_fusion), kind=kOutput, calls=%fused_computation.25 | convolution fusion | flops 1008926720 | bytes 5798016 | tf_op jit(solution)/shard_map/hscr,hscd->hrd/dot_general | solution.py:190
  199.2 2.8 %collective-permute-done.25 = bf16[128,512]{1,0:T(8,128)(2,1)S(1)} collective-permute-done((bf16[128,512]{1,0:T(8,128)(2,1)S(1)}, bf16[128,512]{1,0:T(8,128)(2,1)S(1)}, u32[]{:S(2)}, u32[]{:S(2)}) %collective-permute-start.25) | collective-permute-done | bytes 131104 | tf_op jit(solution)/shard_map/ppermute | solution.py:37
  202.0 2.8 %collective-permute-done.28 = bf16[128,512]{1,0:T(8,128)(2,1)S(1)} collective-permute-done((bf16[128,512]{1,0:T(8,128)(2,1)S(1)}, bf16[128,512]{1,0:T(8,128)(2,1)S(1)}, u32[]{:S(2)}, u32[]{:S(2)}) %collective-permute-start.28) | collective-permute-done | bytes 131104 | tf_op jit(solution)/shard_map/ppermute | solution.py:37
  204.9 1.6 collective-permute-start.29
  208.5 2.7 %collective-permute-done.29 = bf16[128,512]{1,0:T(8,128)(2,1)S(1)} collective-permute-done((bf16[128,512]{1,0:T(8,128)(2,1)S(1)}, bf16[128,512]{1,0:T(8,128)(2,1)S(1)}, u32[]{:S(2)}, u32[]{:S(2)}) %collective-permute-start.29) | collective-permute-done | bytes 131104 | tf_op jit(solution)/shard_map/ppermute | solution.py:37
  211.2 2.5 collective-permute-start.30
  214.3 4.3 %collective-permute-done.30 = bf16[128,512]{1,0:T(8,128)(2,1)S(1)} collective-permute-done((bf16[128,512]{1,0:T(8,128)(2,1)S(1)}, bf16[128,512]{1,0:T(8,128)(2,1)S(1)}, u32[]{:S(2)}, u32[]{:S(2)}) %collective-permute-start.30) | collective-permute-done | bytes 131104 | tf_op jit(solution)/shard_map/ppermute | solution.py:37
  219.6 2.7 %all-gather.11.cloned.1.call-done = bf16[6,512,512]{2,1,0:T(8,128)(2,1)} async-done(((bf16[6,128,512]{2,1,0:T(8,128)(2,1)}), bf16[6,512,512]{2,1,0:T(8,128)(2,1)}) %all-gather.11.cloned.1.call-update) | async-done | bytes 3145744 | tf_op jit(solution)/shard_map/all_gather | solution.py:89
  222.3 4.3 %bitcast_convert_fusion = bf16[8,128,512]{2,1,0:T(8,128)(2,1)} fusion(bf16[6,512,512]{2,1,0:T(8,128)(2,1)} %all-gather.11.cloned.1.call-done, f32[8,6,32]{2,1,0:T(8,128)S(1)} %fusion.48, bf16[8,6,32,512]{3,2,0,1:T(8,128)(2,1)S(1)} %fusion.3, f32[8,6,128]{2,1,0:T(8,128)S(1)} %get-tuple-element.75, f32[32]{0:T(128)S(1)} %iota_convert_fusion), kind=kOutput, calls=%fused_computation.24 | convolution fusion | flops 1008926720 | bytes 5798016 | tf_op jit(solution)/shard_map/hscr,hscd->hrd/dot_general | solution.py:190
  231.4 2.8 %collective-permute-done.32 = bf16[128,512]{1,0:T(8,128)(2,1)S(1)} collective-permute-done((bf16[128,512]{1,0:T(8,128)(2,1)S(1)}, bf16[128,512]{1,0:T(8,128)(2,1)S(1)}, u32[]{:S(2)}, u32[]{:S(2)}) %collective-permute-start.32) | collective-permute-done | bytes 131104 | tf_op jit(solution)/shard_map/ppermute | solution.py:37
  234.3 2.8 %collective-permute-done.35 = bf16[128,512]{1,0:T(8,128)(2,1)S(1)} collective-permute-done((bf16[128,512]{1,0:T(8,128)(2,1)S(1)}, bf16[128,512]{1,0:T(8,128)(2,1)S(1)}, u32[]{:S(2)}, u32[]{:S(2)}) %collective-permute-start.35) | collective-permute-done | bytes 131104 | tf_op jit(solution)/shard_map/ppermute | solution.py:37
  238.1 1.6 collective-permute-start.36
  244.6 2.5 collective-permute-start.37
  247.1 1.6 broadcast_select_fusion
  249.0 1.6 collective-permute-done.37
  (159 shorter events, 48.8 us)
Async XLA Ops:
  7.2 58.3 %copy-start = (bf16[128,1536]{1,0:T(8,128)(2,1)S(1)}, bf16[128,1536]{1,0:T(8,128)(2,1)}, u32[]{:S(2)}) copy-start(bf16[128,1536]{1,0:T(8,128)(2,1)} %param.18) | copy-start | bytes 1179652
  7.2 125.3 %all-gather.5.cloned.1.call-start = ((), (), s32[]{:S(2)}) async-start(), calls=%async_computation | async-start | bytes 23592960 | tf_op jit(solution)/shard_map/all_gather | solution.py:86
  8.0 154.2 %all-gather.7.cloned.1.call-start = ((), (), s32[]{:S(2)}) async-start(), calls=%async_computation.1 | async-start | bytes 3932160 | tf_op jit(solution)/shard_map/all_gather | solution.py:89
  10.4 181.9 %all-gather.9.cloned.1.call-start = ((), (), s32[]{:S(2)}) async-start(), calls=%async_computation.2 | async-start | bytes 3932160 | tf_op jit(solution)/shard_map/all_gather | solution.py:89
  11.1 211.2 %all-gather.11.cloned.1.call-start = ((), (), s32[]{:S(2)}) async-start(), calls=%async_computation.3 | async-start | bytes 3932160 | tf_op jit(solution)/shard_map/all_gather | solution.py:89
  11.2 5.3 %collective-permute-start = (bf16[48,768]{1,0:T(8,128)(2,1)S(1)}, bf16[48,768]{1,0:T(8,128)(2,1)S(1)}, u32[]{:S(2)}, u32[]{:S(2)}) collective-permute-start(bf16[48,768]{1,0:T(8,128)(2,1)S(1)} %slice.171), channel_id=1, source_target_pairs={{0,16},{8,24},{16,0},{24,8},{1,17},{9,25},{17,1},{25,9},{2,18},{10... | collective-permute-start | bytes 221192 | tf_op jit(solution)/shard_map/ppermute | solution.py:26
  16.7 4.8 %collective-permute-start.5 = (bf16[48,896]{1,0:T(8,128)(2,1)S(1)}, bf16[48,896]{1,0:T(8,128)(2,1)S(1)}, u32[]{:S(2)}, u32[]{:S(2)}) collective-permute-start(bf16[48,896]{1,0:T(8,128)(2,1)S(1)} %concatenate.12), channel_id=1, source_target_pairs={{0,16},{8,24},{16,0},{24,8},{1,17},{9,25},{17,1},{25,9},{2,18},{10... | collective-permute-start | bytes 258056 | tf_op jit(solution)/shard_map/ppermute | solution.py:26
  18.8 8.3 %collective-permute-start.1 = (bf16[2,48,768]{2,1,0:T(8,128)(2,1)S(1)}, bf16[2,48,768]{2,1,0:T(8,128)(2,1)S(1)}, u32[]{:S(2)}, u32[]{:S(2)}) collective-permute-start(bf16[2,48,768]{2,1,0:T(8,128)(2,1)S(1)} %pad_maximum_fusion.10), channel_id=1, source_target_pairs={{0,4},{1,5},{2,6},{3,7},{4,0},{5,1},{6,2},{7,3},{8,12},{9,13},{10,... | collective-permute-start | bytes 442376 | tf_op jit(solution)/shard_map/ppermute | solution.py:26
  21.5 6.4 %collective-permute-start.6 = (bf16[2,48,896]{2,1,0:T(8,128)(2,1)S(1)}, bf16[2,48,896]{2,1,0:T(8,128)(2,1)S(1)}, u32[]{:S(2)}, u32[]{:S(2)}) collective-permute-start(bf16[2,48,896]{2,1,0:T(8,128)(2,1)S(1)} %pad_maximum_fusion.9), channel_id=1, source_target_pairs={{0,1},{1,0},{2,3},{3,2},{4,5},{5,4},{6,7},{7,6},{8,9},{9,8},{10,11... | collective-permute-start | bytes 516104 | tf_op jit(solution)/shard_map/ppermute | solution.py:26
  27.1 12.8 %collective-permute-start.2 = (bf16[2,2,48,768]{3,2,1,0:T(8,128)(2,1)S(1)}, bf16[2,2,48,768]{3,2,1,0:T(8,128)(2,1)S(1)}, u32[]{:S(2)}, u32[]{:S(2)}) collective-permute-start(bf16[2,2,48,768]{3,2,1,0:T(8,128)(2,1)S(1)} %pad_maximum_fusion.8), channel_id=1, source_target_pairs={{0,2},{1,3},{2,0},{3,1},{4,6},{5,7},{6,4},{7,5},{8,10},{9,11},{10,... | collective-permute-start | bytes 884744 | tf_op jit(solution)/shard_map/ppermute | solution.py:26
  27.9 17.9 %collective-permute-start.7 = (bf16[2,2,48,896]{3,2,1,0:T(8,128)(2,1)S(1)}, bf16[2,2,48,896]{3,2,1,0:T(8,128)(2,1)S(1)}, u32[]{:S(2)}, u32[]{:S(2)}) collective-permute-start(bf16[2,2,48,896]{3,2,1,0:T(8,128)(2,1)S(1)} %pad_maximum_fusion.7), channel_id=1, source_target_pairs={{0,4},{1,5},{2,6},{3,7},{4,0},{5,1},{6,2},{7,3},{8,12},{9,13},{10,... | collective-permute-start | bytes 1032200 | tf_op jit(solution)/shard_map/ppermute | solution.py:26
  40.0 9.9 %collective-permute-start.3 = (bf16[2,2,2,48,768]{4,3,2,1,0:T(8,128)(2,1)S(1)}, bf16[2,2,2,48,768]{4,3,2,1,0:T(8,128)(2,1)S(1)}, u32[]{:S(2)}, u32[]{:S(2)}) collective-permute-start(bf16[2,2,2,48,768]{4,3,2,1,0:T(8,128)(2,1)S(1)} %pad_maximum_fusion.6), channel_id=1, source_target_pairs={{0,1},{1,0},{2,3},{3,2},{4,5},{5,4},{6,7},{7,6},{8,9},{9,8},{10,11... | collective-permute-start | bytes 1769480 | tf_op jit(solution)/shard_map/ppermute | solution.py:26
  46.0 14.5 %collective-permute-start.8 = (bf16[2,2,2,48,896]{4,3,2,1,0:T(8,128)(2,1)S(1)}, bf16[2,2,2,48,896]{4,3,2,1,0:T(8,128)(2,1)S(1)}, u32[]{:S(2)}, u32[]{:S(2)}) collective-permute-start(bf16[2,2,2,48,896]{4,3,2,1,0:T(8,128)(2,1)S(1)} %pad_maximum_fusion.5), channel_id=1, source_target_pairs={{0,2},{1,3},{2,0},{3,1},{4,6},{5,7},{6,4},{7,5},{8,10},{9,11},{10,... | collective-permute-start | bytes 2064392 | tf_op jit(solution)/shard_map/ppermute | solution.py:26
  51.2 12.6 %collective-permute-start.4 = (bf16[2,2,2,2,48,768]{5,4,3,2,1,0:T(8,128)(2,1)}, bf16[2,2,2,2,48,768]{5,4,3,2,1,0:T(8,128)(2,1)}, u32[]{:S(2)}, u32[]{:S(2)}) collective-permute-start(bf16[2,2,2,2,48,768]{5,4,3,2,1,0:T(8,128)(2,1)} %pad_maximum_fusion.3), channel_id=1, source_target_pairs={{0,8},{8,0},{16,24},{24,16},{1,9},{9,1},{17,25},{25,17},{2,10},{10... | collective-permute-start | bytes 3538952 | tf_op jit(solution)/shard_map/ppermute | solution.py:26
  51.9 11.9 %copy-start.9 = (s32[128,8]{0,1:T(8,128)S(1)}, s32[128,8]{0,1:T(8,128)}, u32[]{:S(2)}) copy-start(s32[128,8]{0,1:T(8,128)} %param.28) | copy-start | bytes 12292
  51.9 11.9 %copy-start.10 = (s32[128,8]{0,1:T(8,128)S(1)}, s32[128,8]{0,1:T(8,128)}, u32[]{:S(2)}) copy-start(s32[128,8]{0,1:T(8,128)} %param.27) | copy-start | bytes 12292
  61.8 4.5 %collective-permute-start.9 = (bf16[2,2,2,2,48,896]{5,4,3,2,1,0:T(8,128)(2,1)}, bf16[2,2,2,2,48,896]{5,4,3,2,1,0:T(8,128)(2,1)}, u32[]{:S(2)}, u32[]{:S(2)}) collective-permute-start(bf16[2,2,2,2,48,896]{5,4,3,2,1,0:T(8,128)(2,1)} %pad_maximum_fusion.2), channel_id=1, source_target_pairs={{0,8},{8,0},{16,24},{24,16},{1,9},{9,1},{17,25},{25,17},{2,10},{10... | collective-permute-start | bytes 4128776 | tf_op jit(solution)/shard_map/ppermute | solution.py:26
  76.6 28.3 %collective-permute-start.10 = (bf16[128,1792]{0,1:T(8,128)(2,1)S(1)}, bf16[128,1792]{0,1:T(8,128)(2,1)S(1)}, u32[]{:S(2)}, u32[]{:S(2)}) collective-permute-start(bf16[128,1792]{0,1:T(8,128)(2,1)S(1)} %constant_dynamic-update-slice_fusion), channel_id=1, source_target_pairs={{0,1},{1,0},{2,3},{3,2},{4,5},{5,4},{6,7},{7,6},{8,9},{9,8},{10,11... | collective-permute-start | bytes 1376264 | tf_op jit(solution)/shard_map/ppermute | solution.py:164
  78.2 25.2 %collective-permute-start.11 = (bf16[128,1792]{0,1:T(8,128)(2,1)S(1)}, bf16[128,1792]{0,1:T(8,128)(2,1)S(1)}, u32[]{:S(2)}, u32[]{:S(2)}) collective-permute-start(bf16[128,1792]{0,1:T(8,128)(2,1)S(1)} %constant_dynamic-update-slice_fusion), channel_id=1, source_target_pairs={{0,2},{1,3},{2,0},{3,1},{4,6},{5,7},{6,4},{7,5},{8,10},{9,11},{10,... | collective-permute-start | bytes 1376264 | tf_op jit(solution)/shard_map/ppermute | solution.py:164
  78.6 24.0 %collective-permute-start.13 = (bf16[128,1792]{0,1:T(8,128)(2,1)S(1)}, bf16[128,1792]{0,1:T(8,128)(2,1)S(1)}, u32[]{:S(2)}, u32[]{:S(2)}) collective-permute-start(bf16[128,1792]{0,1:T(8,128)(2,1)S(1)} %constant_dynamic-update-slice_fusion), channel_id=1, source_target_pairs={{0,4},{1,5},{2,6},{3,7},{4,0},{5,1},{6,2},{7,3},{8,12},{9,13},{10,... | collective-permute-start | bytes 1376264 | tf_op jit(solution)/shard_map/ppermute | solution.py:164
  102.6 22.9 %collective-permute-start.14 = (bf16[128,1792]{0,1:T(8,128)(2,1)S(1)}, bf16[128,1792]{0,1:T(8,128)(2,1)S(1)}, u32[]{:S(2)}, u32[]{:S(2)}) collective-permute-start(bf16[128,1792]{0,1:T(8,128)(2,1)S(1)} %collective-permute-done.13), channel_id=1, source_target_pairs={{0,1},{1,0},{2,3},{3,2},{4,5},{5,4},{6,7},{7,6},{8,9},{9,8},{10,11... | collective-permute-start | bytes 1376264 | tf_op jit(solution)/shard_map/ppermute | solution.py:164
  103.0 10.2 %collective-permute-start.15 = (bf16[128,1792]{0,1:T(8,128)(2,1)S(1)}, bf16[128,1792]{0,1:T(8,128)(2,1)S(1)}, u32[]{:S(2)}, u32[]{:S(2)}) collective-permute-start(bf16[128,1792]{0,1:T(8,128)(2,1)S(1)} %collective-permute-done.13), channel_id=1, source_target_pairs={{0,2},{1,3},{2,0},{3,1},{4,6},{5,7},{6,4},{7,5},{8,10},{9,11},{10,... | collective-permute-start | bytes 1376264 | tf_op jit(solution)/shard_map/ppermute | solution.py:164
  103.4 22.0 %collective-permute-start.12 = (bf16[128,1792]{0,1:T(8,128)(2,1)S(1)}, bf16[128,1792]{0,1:T(8,128)(2,1)S(1)}, u32[]{:S(2)}, u32[]{:S(2)}) collective-permute-start(bf16[128,1792]{0,1:T(8,128)(2,1)S(1)} %collective-permute-done.11), channel_id=1, source_target_pairs={{0,1},{1,0},{2,3},{3,2},{4,5},{5,4},{6,7},{7,6},{8,9},{9,8},{10,11... | collective-permute-start | bytes 1376264 | tf_op jit(solution)/shard_map/ppermute | solution.py:164
  113.2 17.0 %collective-permute-start.16 = (bf16[128,1792]{0,1:T(8,128)(2,1)S(1)}, bf16[128,1792]{0,1:T(8,128)(2,1)S(1)}, u32[]{:S(2)}, u32[]{:S(2)}) collective-permute-start(bf16[128,1792]{0,1:T(8,128)(2,1)S(1)} %collective-permute-done.15), channel_id=1, source_target_pairs={{0,1},{1,0},{2,3},{3,2},{4,5},{5,4},{6,7},{7,6},{8,9},{9,8},{10,11... | collective-permute-start | bytes 1376264 | tf_op jit(solution)/shard_map/ppermute | solution.py:164
  165.5 6.4 %collective-permute-start.18 = (bf16[128,512]{1,0:T(8,128)(2,1)S(1)}, bf16[128,512]{1,0:T(8,128)(2,1)S(1)}, u32[]{:S(2)}, u32[]{:S(2)}) collective-permute-start(bf16[128,512]{1,0:T(8,128)(2,1)S(1)} %get-tuple-element.59), channel_id=1, source_target_pairs={{0,1},{1,0},{2,3},{3,2},{4,5},{5,4},{6,7},{7,6},{8,9},{9,8},{10,11... | collective-permute-start | bytes 393224 | tf_op jit(solution)/shard_map/ppermute | solution.py:37
  167.0 7.7 %collective-permute-start.21 = (bf16[128,512]{1,0:T(8,128)(2,1)S(1)}, bf16[128,512]{1,0:T(8,128)(2,1)S(1)}, u32[]{:S(2)}, u32[]{:S(2)}) collective-permute-start(bf16[128,512]{1,0:T(8,128)(2,1)S(1)} %get-tuple-element.57), channel_id=1, source_target_pairs={{0,1},{1,0},{2,3},{3,2},{4,5},{5,4},{6,7},{7,6},{8,9},{9,8},{10,11... | collective-permute-start | bytes 393224 | tf_op jit(solution)/shard_map/ppermute | solution.py:37
  167.6 10.8 %collective-permute-start.20 = (bf16[128,512]{1,0:T(8,128)(2,1)S(1)}, bf16[128,512]{1,0:T(8,128)(2,1)S(1)}, u32[]{:S(2)}, u32[]{:S(2)}) collective-permute-start(bf16[128,512]{1,0:T(8,128)(2,1)S(1)} %get-tuple-element.58), channel_id=1, source_target_pairs={{0,1},{1,0},{2,3},{3,2},{4,5},{5,4},{6,7},{7,6},{8,9},{9,8},{10,11... | collective-permute-start | bytes 393224 | tf_op jit(solution)/shard_map/ppermute | solution.py:37
  174.8 6.3 %collective-permute-start.22 = (bf16[128,512]{1,0:T(8,128)(2,1)S(1)}, bf16[128,512]{1,0:T(8,128)(2,1)S(1)}, u32[]{:S(2)}, u32[]{:S(2)}) collective-permute-start(bf16[128,512]{1,0:T(8,128)(2,1)S(1)} %get-tuple-element.61), channel_id=1, source_target_pairs={{0,2},{1,3},{2,0},{3,1},{4,6},{5,7},{6,4},{7,5},{8,10},{9,11},{10,... | collective-permute-start | bytes 393224 | tf_op jit(solution)/shard_map/ppermute | solution.py:37
  176.3 7.3 %collective-permute-start.17 = (bf16[128,512]{1,0:T(8,128)(2,1)S(1)}, bf16[128,512]{1,0:T(8,128)(2,1)S(1)}, u32[]{:S(2)}, u32[]{:S(2)}) collective-permute-start(bf16[128,512]{1,0:T(8,128)(2,1)S(1)} %get-tuple-element.56), channel_id=1, source_target_pairs={{0,1},{1,0},{2,3},{3,2},{4,5},{5,4},{6,7},{7,6},{8,9},{9,8},{10,11... | collective-permute-start | bytes 393224 | tf_op jit(solution)/shard_map/ppermute | solution.py:37
  177.8 6.4 %collective-permute-start.19 = (bf16[128,512]{1,0:T(8,128)(2,1)S(1)}, bf16[128,512]{1,0:T(8,128)(2,1)S(1)}, u32[]{:S(2)}, u32[]{:S(2)}) collective-permute-start(bf16[128,512]{1,0:T(8,128)(2,1)S(1)} %get-tuple-element.60), channel_id=1, source_target_pairs={{0,2},{1,3},{2,0},{3,1},{4,6},{5,7},{6,4},{7,5},{8,10},{9,11},{10,... | collective-permute-start | bytes 393224 | tf_op jit(solution)/shard_map/ppermute | solution.py:37
  181.1 7.3 %collective-permute-start.23 = (bf16[128,512]{1,0:T(8,128)(2,1)S(1)}, bf16[128,512]{1,0:T(8,128)(2,1)S(1)}, u32[]{:S(2)}, u32[]{:S(2)}) collective-permute-start(bf16[128,512]{1,0:T(8,128)(2,1)S(1)} %add_convert_fusion.4), channel_id=1, source_target_pairs={{0,4},{1,5},{2,6},{3,7},{4,0},{5,1},{6,2},{7,3},{8,12},{9,13},{10,... | collective-permute-start | bytes 393224 | tf_op jit(solution)/shard_map/ppermute | solution.py:37
  195.6 18.7 %copy-start.4 = (bf16[8,128,512]{2,1,0:T(8,128)(2,1)}, bf16[8,128,512]{2,1,0:T(8,128)(2,1)S(1)}, u32[]{:S(2)}) copy-start(bf16[8,128,512]{2,1,0:T(8,128)(2,1)S(1)} %bitcast_convert_fusion.1) | copy-start | bytes 3145732
  195.6 6.4 %collective-permute-start.25 = (bf16[128,512]{1,0:T(8,128)(2,1)S(1)}, bf16[128,512]{1,0:T(8,128)(2,1)S(1)}, u32[]{:S(2)}, u32[]{:S(2)}) collective-permute-start(bf16[128,512]{1,0:T(8,128)(2,1)S(1)} %get-tuple-element.53), channel_id=1, source_target_pairs={{0,1},{1,0},{2,3},{3,2},{4,5},{5,4},{6,7},{7,6},{8,9},{9,8},{10,11... | collective-permute-start | bytes 393224 | tf_op jit(solution)/shard_map/ppermute | solution.py:37
  197.2 7.7 %collective-permute-start.28 = (bf16[128,512]{1,0:T(8,128)(2,1)S(1)}, bf16[128,512]{1,0:T(8,128)(2,1)S(1)}, u32[]{:S(2)}, u32[]{:S(2)}) collective-permute-start(bf16[128,512]{1,0:T(8,128)(2,1)S(1)} %get-tuple-element.51), channel_id=1, source_target_pairs={{0,1},{1,0},{2,3},{3,2},{4,5},{5,4},{6,7},{7,6},{8,9},{9,8},{10,11... | collective-permute-start | bytes 393224 | tf_op jit(solution)/shard_map/ppermute | solution.py:37
  197.7 10.7 %collective-permute-start.27 = (bf16[128,512]{1,0:T(8,128)(2,1)S(1)}, bf16[128,512]{1,0:T(8,128)(2,1)S(1)}, u32[]{:S(2)}, u32[]{:S(2)}) collective-permute-start(bf16[128,512]{1,0:T(8,128)(2,1)S(1)} %get-tuple-element.52), channel_id=1, source_target_pairs={{0,1},{1,0},{2,3},{3,2},{4,5},{5,4},{6,7},{7,6},{8,9},{9,8},{10,11... | collective-permute-start | bytes 393224 | tf_op jit(solution)/shard_map/ppermute | solution.py:37
  204.9 6.3 %collective-permute-start.29 = (bf16[128,512]{1,0:T(8,128)(2,1)S(1)}, bf16[128,512]{1,0:T(8,128)(2,1)S(1)}, u32[]{:S(2)}, u32[]{:S(2)}) collective-permute-start(bf16[128,512]{1,0:T(8,128)(2,1)S(1)} %get-tuple-element.55), channel_id=1, source_target_pairs={{0,2},{1,3},{2,0},{3,1},{4,6},{5,7},{6,4},{7,5},{8,10},{9,11},{10,... | collective-permute-start | bytes 393224 | tf_op jit(solution)/shard_map/ppermute | solution.py:37
  206.5 7.3 %collective-permute-start.24 = (bf16[128,512]{1,0:T(8,128)(2,1)S(1)}, bf16[128,512]{1,0:T(8,128)(2,1)S(1)}, u32[]{:S(2)}, u32[]{:S(2)}) collective-permute-start(bf16[128,512]{1,0:T(8,128)(2,1)S(1)} %get-tuple-element.50), channel_id=1, source_target_pairs={{0,1},{1,0},{2,3},{3,2},{4,5},{5,4},{6,7},{7,6},{8,9},{9,8},{10,11... | collective-permute-start | bytes 393224 | tf_op jit(solution)/shard_map/ppermute | solution.py:37
  207.9 6.4 %collective-permute-start.26 = (bf16[128,512]{1,0:T(8,128)(2,1)S(1)}, bf16[128,512]{1,0:T(8,128)(2,1)S(1)}, u32[]{:S(2)}, u32[]{:S(2)}) collective-permute-start(bf16[128,512]{1,0:T(8,128)(2,1)S(1)} %get-tuple-element.54), channel_id=1, source_target_pairs={{0,2},{1,3},{2,0},{3,1},{4,6},{5,7},{6,4},{7,5},{8,10},{9,11},{10,... | collective-permute-start | bytes 393224 | tf_op jit(solution)/shard_map/ppermute | solution.py:37
  211.2 7.3 %collective-permute-start.30 = (bf16[128,512]{1,0:T(8,128)(2,1)S(1)}, bf16[128,512]{1,0:T(8,128)(2,1)S(1)}, u32[]{:S(2)}, u32[]{:S(2)}) collective-permute-start(bf16[128,512]{1,0:T(8,128)(2,1)S(1)} %add_convert_fusion.2), channel_id=1, source_target_pairs={{0,4},{1,5},{2,6},{3,7},{4,0},{5,1},{6,2},{7,3},{8,12},{9,13},{10,... | collective-permute-start | bytes 393224 | tf_op jit(solution)/shard_map/ppermute | solution.py:37
  219.5 27.6 %copy-start.6 = (bf16[128,1024]{1,0:T(8,128)(2,1)S(1)}, bf16[128,1024]{1,0:T(8,128)(2,1)}, u32[]{:S(2)}) copy-start(bf16[128,1024]{1,0:T(8,128)(2,1)} %param.20) | copy-start | bytes 786436
  226.6 20.5 %copy-start.3 = (bf16[8,128,1024]{2,1,0:T(8,128)(2,1)S(1)}, bf16[8,128,1024]{2,1,0:T(8,128)(2,1)}, u32[]{:S(2)}) copy-start(bf16[8,128,1024]{2,1,0:T(8,128)(2,1)} %param.21) | copy-start | bytes 6291460
  227.9 6.4 %collective-permute-start.32 = (bf16[128,512]{1,0:T(8,128)(2,1)S(1)}, bf16[128,512]{1,0:T(8,128)(2,1)S(1)}, u32[]{:S(2)}, u32[]{:S(2)}) collective-permute-start(bf16[128,512]{1,0:T(8,128)(2,1)S(1)} %get-tuple-element.47), channel_id=1, source_target_pairs={{0,1},{1,0},{2,3},{3,2},{4,5},{5,4},{6,7},{7,6},{8,9},{9,8},{10,11... | collective-permute-start | bytes 393224 | tf_op jit(solution)/shard_map/ppermute | solution.py:37
  229.4 7.7 %collective-permute-start.35 = (bf16[128,512]{1,0:T(8,128)(2,1)S(1)}, bf16[128,512]{1,0:T(8,128)(2,1)S(1)}, u32[]{:S(2)}, u32[]{:S(2)}) collective-permute-start(bf16[128,512]{1,0:T(8,128)(2,1)S(1)} %get-tuple-element.45), channel_id=1, source_target_pairs={{0,1},{1,0},{2,3},{3,2},{4,5},{5,4},{6,7},{7,6},{8,9},{9,8},{10,11... | collective-permute-start | bytes 393224 | tf_op jit(solution)/shard_map/ppermute | solution.py:37
  230.0 12.4 %collective-permute-start.34 = (bf16[128,512]{1,0:T(8,128)(2,1)S(1)}, bf16[128,512]{1,0:T(8,128)(2,1)S(1)}, u32[]{:S(2)}, u32[]{:S(2)}) collective-permute-start(bf16[128,512]{1,0:T(8,128)(2,1)S(1)} %get-tuple-element.46), channel_id=1, source_target_pairs={{0,1},{1,0},{2,3},{3,2},{4,5},{5,4},{6,7},{7,6},{8,9},{9,8},{10,11... | collective-permute-start | bytes 393224 | tf_op jit(solution)/shard_map/ppermute | solution.py:37
  238.1 5.6 %collective-permute-start.36 = (bf16[128,512]{1,0:T(8,128)(2,1)S(1)}, bf16[128,512]{1,0:T(8,128)(2,1)S(1)}, u32[]{:S(2)}, u32[]{:S(2)}) collective-permute-start(bf16[128,512]{1,0:T(8,128)(2,1)S(1)} %get-tuple-element.49), channel_id=1, source_target_pairs={{0,2},{1,3},{2,0},{3,1},{4,6},{5,7},{6,4},{7,5},{8,10},{9,11},{10,... | collective-permute-start | bytes 393224 | tf_op jit(solution)/shard_map/ppermute | solution.py:37
  240.3 8.6 %collective-permute-start.31 = (bf16[128,512]{1,0:T(8,128)(2,1)S(1)}, bf16[128,512]{1,0:T(8,128)(2,1)S(1)}, u32[]{:S(2)}, u32[]{:S(2)}) collective-permute-start(bf16[128,512]{1,0:T(8,128)(2,1)S(1)} %get-tuple-element.44), channel_id=1, source_target_pairs={{0,1},{1,0},{2,3},{3,2},{4,5},{5,4},{6,7},{7,6},{8,9},{9,8},{10,11... | collective-permute-start | bytes 393224 | tf_op jit(solution)/shard_map/ppermute | solution.py:37
  241.9 7.1 %collective-permute-start.33 = (bf16[128,512]{1,0:T(8,128)(2,1)S(1)}, bf16[128,512]{1,0:T(8,128)(2,1)S(1)}, u32[]{:S(2)}, u32[]{:S(2)}) collective-permute-start(bf16[128,512]{1,0:T(8,128)(2,1)S(1)} %get-tuple-element.48), channel_id=1, source_target_pairs={{0,2},{1,3},{2,0},{3,1},{4,6},{5,7},{6,4},{7,5},{8,10},{9,11},{10,... | collective-permute-start | bytes 393224 | tf_op jit(solution)/shard_map/ppermute | solution.py:37
  244.6 5.9 %collective-permute-start.37 = (bf16[128,512]{1,0:T(8,128)(2,1)S(1)}, bf16[128,512]{1,0:T(8,128)(2,1)S(1)}, u32[]{:S(2)}, u32[]{:S(2)}) collective-permute-start(bf16[128,512]{1,0:T(8,128)(2,1)S(1)} %add_convert_fusion), channel_id=1, source_target_pairs={{0,4},{1,5},{2,6},{3,7},{4,0},{5,1},{6,2},{7,3},{8,12},{9,13},{10,... | collective-permute-start | bytes 393224 | tf_op jit(solution)/shard_map/ppermute | solution.py:37
  (10 other events, 51.5 us)
Sparse Core Ops, SparseCore 0:
  9.6 122.3 all-gather.4
  133.6 28.5 all-gather.6
  163.7 28.5 all-gather.8
  193.7 28.5 all-gather.10
